TPU v7x, 256 devices: a whole 4x4x8 slice. The times are simulated.
256 devices in a mesh: upd: 8 (over x, core), col: 32 (over z, y).
Axes of the slice: x: 4, y: 4, z: 8, core: 2. Of those that a mesh axis runs over, the one named last changes fastest.
Arguments:
- panel: bfloat16 [32, 8, 1024, 1024], P('col', None, 'upd'), may hold values from -6 to 6
- diag_tiles: bfloat16 [32, 1024, 1024], P('col', 'upd'), may hold values from -6 to 6
- dinv: bfloat16 [32, 1024, 1024], P('col'), may hold values from -1 to 1, as said below
- u_fac: bfloat16 [32, 8, 8, 96, 1024], P('col', None, 'upd'), may hold values from -1.1953125 to 1.1953125
- v_fac: bfloat16 [32, 8, 8, 96, 1024], P('col', None, 'upd'), may hold values from -1.1953125 to 1.1953125
- ranks: int32 [32, 8, 8], P('col', None, 'upd'), may hold values from 1 to 96, as said below
- sketch: bfloat16 [32, 64, 1024], P('col'), may hold values from -6 to 6
Outputs:
- panel_out: bfloat16 [32, 8, 1024, 1024], P('col', None, 'upd')
- diag_out: float32 [32, 1024, 1024], P('col', 'upd')
Inputs may be any that keep to these rules, and one draw needn't show every extreme that they name: `ranks`: in every panel tile at least two of the 8 pieces have rank 96. `dinv`: each block is lower triangular with a positive diagonal.
All inputs are finite; a program needn't handle non-finite values.
Results may differ from a plain program's by a relative error of at most 0.014.
Values may be sent and summed in bfloat16 or wider, within the bound.
No kernel may reach another device: no remote copies, remote signals or barrier semaphores. Data moves between devices by JAX's collectives and lax.ppermute only.
A program may use at most 64 MiB of HBM per device.

v0:
```python
import jax
import jax.numpy as jnp
from jax import lax
from jax.experimental import pallas as pl
from jax.experimental.pallas import tpu as pltpu
from jax.sharding import PartitionSpec as P


F32 = jnp.float32
BF16 = jnp.bfloat16
AXES = ("upd", "col")
NU = 8
NX = 4
NY = 4
NZ = 8
NC = 32
HALF = 5
BLK = 128
NEAR = ((1,), (1,))
LEFT = ((0,), (0,))
EXACT = lax.Precision.HIGHEST


def dot(a, b, dims, precision=None):
    return lax.dot_general(a, b, (dims, ((), ())), precision=precision, preferred_element_type=F32)


def place():
    at = lax.axis_index("upd")
    return at >> 1, at & 1


def perm(block, route):
    pairs = []
    for u in range(NU):
        for c in range(NC):
            to = route(u, c)
            if to is not None:
                pairs.append((u * NC + c, to[0] * NC + to[1]))
    return lax.ppermute(block, AXES, pairs)


def along_x(k):
    return lambda u, c: ((u + 2 * k) % NU, c)


def along_upd(k):
    return lambda u, c: ((u + k) % NU, c)


def partner(u, c):
    return (u ^ 1, c)


def to_column(k, other):
    def route(u, c):
        x, core = u // 2, u % 2
        plane, y = c // NY, c % NY
        return (2 * ((x + k) % NX) + (core ^ other), (plane + core) % NZ * NY + (y + x + 1) % NY)

    return route


def along_z(k):
    return lambda u, c: (u, (c + NY * k) % NC)


def call(kernel, outs, ins, scalars=(), scratch=(), in_hbm=False):
    vmem = pl.BlockSpec(memory_space=pltpu.VMEM)
    if in_hbm:
        shapes = [jax.ShapeDtypeStruct(*out) for out in outs]
    else:
        shapes = [pltpu.VMEM(*out) for out in outs]
    out_spec = pl.BlockSpec(memory_space=pl.ANY) if in_hbm else vmem
    return pl.pallas_call(
        kernel,
        out_shape=shapes,
        in_specs=[pl.BlockSpec(memory_space=pltpu.SMEM)] * len(scalars) + [vmem] * len(ins),
        out_specs=[out_spec] * len(outs),
        scratch_shapes=list(scratch),
        compiler_params=pltpu.CompilerParams(vmem_limit_bytes=16 * 1024 * 1024),
    )(*scalars, *[pltpu.with_memory_space_constraint(x, pltpu.VMEM) for x in ins])


def masked(probe, rank):
    slots = lax.broadcasted_iota(jnp.int32, probe.shape, 0)
    return jnp.where(slots < rank, probe, 0.0).astype(BF16)


def sketch_kernel(ranks, v_hbm, u_hbm, sketch_hbm, send_ref, keep_ref, v_ref, u_ref, sketch_ref, sems):
    x, core = place()
    order = [(k, other) for k in range(NX) for other in (1, 0)]
    tiles = [((x + k) & 3) + 4 * (core ^ other) for k, other in order]
    first = pltpu.make_async_copy(sketch_hbm, sketch_ref, sems.at[2 * NU])
    first.start()
    copies = []
    for i, tile in enumerate(tiles):
        pair = (
            pltpu.make_async_copy(v_hbm.at[tile], v_ref.at[i], sems.at[2 * i]),
            pltpu.make_async_copy(u_hbm.at[tile], u_ref.at[i], sems.at[2 * i + 1]),
        )
        for copy in pair:
            copy.start()
        copies.append(pair)
    first.wait()
    for i, (k, other) in enumerate(order):
        copies[i][0].wait()
        probe = masked(dot(v_ref[i], sketch_ref[...], NEAR), ranks[tiles[i]])
        copies[i][1].wait()
        out = dot(probe, u_ref[i], LEFT)
        if other:
            send_ref[k] = out.astype(BF16)
        else:
            keep_ref[k] = out


def sketch_call(ranks, v, u, sketch):
    vmem = pl.BlockSpec(memory_space=pltpu.VMEM)
    hbm = pl.BlockSpec(memory_space=pltpu.HBM)
    out = (NX,) + sketch.shape
    return pl.pallas_call(
        sketch_kernel,
        out_shape=[pltpu.VMEM(out, BF16), pltpu.VMEM(out, F32)],
        in_specs=[pl.BlockSpec(memory_space=pltpu.SMEM)] + [hbm] * 3,
        out_specs=[vmem] * 2,
        scratch_shapes=[
            pltpu.VMEM(v.shape, BF16),
            pltpu.VMEM(u.shape, BF16),
            pltpu.VMEM(sketch.shape, BF16),
            pltpu.SemaphoreType.DMA((2 * NU + 1,)),
        ],
        compiler_params=pltpu.CompilerParams(vmem_limit_bytes=16 * 1024 * 1024),
        name="sketch_product",
    )(ranks, *[pltpu.with_memory_space_constraint(x, pltpu.HBM) for x in (v, u, sketch)])


def project_kernel(ranks, u_ref, v_ref, *refs):
    bases, (send_ref, keep_ref) = refs[: NX + 1], refs[NX + 1 :]
    x, core = place()
    for d in range(NX):
        for other in range(2):
            tile = ((x - d) & 3) + 4 * (core ^ other)
            basis = from_source(bases, d, other)[...]
            coeff = masked(dot(u_ref[tile], basis, NEAR), ranks[tile])
            out = dot(coeff, v_ref[tile], LEFT)
            if other:
                send_ref[-d % NX] = out.astype(BF16)
            else:
                keep_ref[-d % NX] = out


def stack_kernel(a_ref, b_ref, c_ref, d_ref, out_ref):
    for k, ref in enumerate((a_ref, b_ref, c_ref, d_ref)):
        out_ref[k] = ref[...]


def stacked(blocks):
    return call(stack_kernel, [((NX,) + blocks[0].shape, BF16)], blocks)[0]


def from_source(refs, d, other):
    return refs[NX].at[d] if other else refs[d]


def sum_product(split, ranks, u, v, sums):
    return call(project_kernel, split, [u, v, *sums], [ranks])


def pair_sum_kernel(keep_ref, got_ref, own_ref, a_ref, b_ref, c_ref):
    for k, ref in enumerate((own_ref, a_ref, b_ref, c_ref)):
        ref[...] = (keep_ref[k] + got_ref[k].astype(F32)).astype(ref.dtype)


def pair_sum(keep, got):
    shape = keep.shape[1:]
    outs = [(shape, F32)] + [(shape, BF16)] * (NX - 1)
    return call(pair_sum_kernel, outs, [keep, got])


def owner_sum(own_ref, *others):
    total = own_ref[...]
    for ref in others:
        total = total + ref[...].astype(F32)
    return total


def summed_kernel(own_ref, a_ref, b_ref, c_ref, summed_ref):
    summed_ref[...] = owner_sum(own_ref, a_ref, b_ref, c_ref).astype(BF16)


def owner_total(own, others):
    return call(summed_kernel, [(own.shape, BF16)], [own, *others])[0]


def inverse_kernel(summed_ref, inverse_ref):
    summed = summed_ref[...].astype(F32)
    rk = summed.shape[0]
    gram = dot(summed, summed, NEAR, EXACT)
    rows = lax.broadcasted_iota(jnp.int32, (rk, rk), 0)
    cols = lax.broadcasted_iota(jnp.int32, (rk, rk), 1)
    row_at = lax.broadcasted_iota(jnp.int32, (rk, 1), 0)
    work = jnp.concatenate([gram, jnp.where(rows == cols, 1.0, 0.0)], axis=1)
    for k in range(rk):
        row = work[k : k + 1, :]
        scaled = row * (1.0 / work[k : k + 1, k : k + 1])
        col = jnp.where(row_at > k, work[:, k : k + 1], 0.0)
        work = work - col * scaled
    pivots = jnp.sum(jnp.where(rows == cols, work[:, :rk], 0.0), axis=1, keepdims=True)
    half = work[:, rk:] * lax.rsqrt(pivots)
    inverse_ref[...] = dot(half, half, LEFT, EXACT)


def gram_inverse(summed):
    rk = summed.shape[0]
    return call(inverse_kernel, [((rk, rk), F32)], [summed])[0]


def split_kernel(panel_ref, send_ref, keep_ref):
    x, core = place()
    for k in range(NX):
        tile = (x + k) & 3
        send_ref[k] = panel_ref[tile + 4 * (core ^ 1)]
        keep_ref[k] = panel_ref[tile + 4 * core]


def bundle_kernel(keep_ref, got_ref, *outs):
    for k, ref in enumerate(outs):
        ref[0] = keep_ref[NX - len(outs) + k]
        ref[1] = got_ref[NX - len(outs) + k]


def bundles(keep, got, first):
    shape = ((2,) + keep.shape[1:], BF16)
    return call(bundle_kernel, [shape] * (NX - first), [keep, got])


def split_panel(panel):
    shape = ((NX,) + panel.shape[1:], BF16)
    return call(split_kernel, [shape] * 2, [panel])


def tile_kernel(sum_ref, inverse_ref, own_ref, a_ref, b_ref, c_ref, dinv_ref, *refs):
    bundles, cross_ref, outs = refs[:5], refs[5], refs[6 : 6 + NU]
    updated, solved = refs[6 + NU :]
    x, core = place()
    raw = owner_sum(own_ref, a_ref, b_ref, c_ref)
    cross_ref[...] = dot(inverse_ref[...], raw, ((1,), (0,)), EXACT).astype(BF16)
    wrap = (HALF - 1) * BLK
    for d in range(NX):
        pair = ((x - d) & 3) * (2 * BLK)
        for other in range(2):
            part = (core ^ other) * BLK
            at = pl.multiple_of(pair + part, BLK)
            rows = bundles[d + 1][other] if d else bundles[other][0]
            lowrank = dot(sum_ref[:, pl.ds(at, BLK)], cross_ref[...], LEFT)
            row_block = (rows.astype(F32) - lowrank).astype(BF16)
            updated[d, pl.ds(pl.multiple_of(part, BLK), BLK)] = row_block
        result = dot(updated[d], dinv_ref[...], NEAR).astype(BF16)
        solved[pl.ds(pl.multiple_of(pair + wrap, 2 * BLK), 2 * BLK)] = result
    solved[:wrap] = solved[-wrap:]
    for k in range(NX):
        at = pl.multiple_of(((x + k) & 3) * (2 * BLK), 2 * BLK)
        product = dot(solved[pl.ds(at + wrap, 2 * BLK)], solved[pl.ds(at, (HALF + 1) * BLK)], NEAR)
        upper = product[:BLK, : HALF * BLK].astype(BF16)
        lower = product[BLK:, BLK:].astype(BF16)
        on_lower = core == 1
        outs[2 * k][...] = jnp.where(on_lower, lower, upper)
        outs[2 * k + 1][...] = jnp.where(on_lower, upper, lower)


def tile_call(summed, inverse, parts, dinv, rows):
    width = dinv.shape[0]
    out = ((BLK, HALF * BLK), BF16)
    return call(
        tile_kernel,
        [(summed.shape, BF16)] + [out] * NU,
        [summed, inverse, *parts, dinv, *rows],
        scratch=[
            pltpu.VMEM((NX, 2 * BLK, width), BF16),
            pltpu.VMEM((width + (HALF - 1) * BLK, width), BF16),
        ],
    )


def rows_kernel(panel_ref, dinv_ref, *refs):
    bases, crosses = refs[: NX + 1], refs[NX + 1 : 2 * NX + 2]
    out_ref, updated, solved, sems = refs[2 * NX + 2 :]
    x, core = place()
    at = pl.multiple_of((2 * x + core) * BLK, BLK)
    copies = []
    for d in range(NX):
        for other in range(2):
            tile = ((x - d) & 3) + 4 * (core ^ other)
            part = from_source(bases, d, other)[:, pl.ds(at, BLK)]
            lowrank = dot(part, from_source(crosses, d, other)[...], LEFT)
            rows = (panel_ref[tile].astype(F32) - lowrank).astype(BF16)
            updated[other * BLK : (other + 1) * BLK] = rows
        result = dot(updated[...], dinv_ref[...], NEAR).astype(BF16)
        for other in range(2):
            tile = ((x - d) & 3) + 4 * (core ^ other)
            slot = 2 * d + other
            solved[slot] = result[other * BLK : (other + 1) * BLK]
            copy = pltpu.make_async_copy(solved.at[slot], out_ref.at[tile], sems.at[slot])
            copy.start()
            copies.append(copy)
    for copy in copies:
        copy.wait()


def rows_call(panel, dinv, bases, crosses):
    return call(
        rows_kernel,
        [(panel.shape, BF16)],
        [panel, dinv, *bases, *crosses],
        scratch=[
            pltpu.VMEM((2 * BLK, panel.shape[2]), BF16),
            pltpu.VMEM(panel.shape, BF16),
            pltpu.SemaphoreType.DMA((NU,)),
        ],
        in_hbm=True,
    )[0]


def arrived_kernel(*refs):
    refs, (here_ref, onward_ref) = refs[:NU], refs[NU:]
    x, core = place()
    col = lax.axis_index("col")
    y, z = col & 3, col >> 2
    here, onward = 0.0, 0.0
    for k in range(NX):
        first, second = refs[2 * k][...].astype(F32), refs[2 * k + 1][...].astype(F32)
        near = jnp.where(core == 0, first, second)
        far = jnp.where(core == 0, second, first)
        both = near + jnp.where(z > 0, far, 0.0)
        stays = y > ((x - k) & 3)
        here = here + jnp.where(stays, both, 0.0)
        onward = onward + jnp.where(stays, 0.0, both)
    here_ref[...] = here
    onward_ref[...] = onward.astype(BF16)


def arrived_sum(arrived):
    shape = arrived[0].shape
    return call(arrived_kernel, [(shape, F32), (shape, BF16)], arrived)


def collect_kernel(here_ref, onward_ref, total_ref, a_ref, b_ref, c_ref):
    z = lax.axis_index("col") >> 2
    total = here_ref[...] + jnp.where(z > 0, onward_ref[...].astype(F32), 0.0)
    total_ref[...] = total
    for d, ref in ((1, a_ref), (2, b_ref), (3, c_ref)):
        i = HALF - 1 - d
        ref[...] = total[:, i * BLK : (i + 1) * BLK].T.astype(BF16)


def collect(here, onward):
    outs = [(here.shape, F32)] + [((BLK, BLK), BF16)] * (HALF - 2)
    return call(collect_kernel, outs, [here, *onward])


def diag_kernel(diag_ref, total_ref, a_ref, b_ref, c_ref, out_ref):
    x, core = place()
    u = 2 * x + core
    for i in range(HALF):
        at = pl.ds(pl.multiple_of(((u + i + 4) & 7) * BLK, BLK), BLK)
        out_ref[:, at] = diag_ref[:, at].astype(F32) - total_ref[:, i * BLK : (i + 1) * BLK]
    for d, ref in ((1, a_ref), (2, b_ref), (3, c_ref)):
        at = pl.ds(pl.multiple_of(((u + d) & 7) * BLK, BLK), BLK)
        out_ref[:, at] = diag_ref[:, at].astype(F32) - ref[...].astype(F32)


def diag_call(diag, total, mirrored):
    vmem = pl.BlockSpec(memory_space=pltpu.VMEM)
    ins = [diag, total, *mirrored]
    return pl.pallas_call(
        diag_kernel,
        out_shape=jax.ShapeDtypeStruct(diag.shape, F32),
        in_specs=[vmem] * len(ins),
        out_specs=vmem,
        compiler_params=pltpu.CompilerParams(vmem_limit_bytes=16 * 1024 * 1024),
        name="diagonal",
    )(*[pltpu.with_memory_space_constraint(x, pltpu.VMEM) for x in ins])


def shifted(blocks, route, first=1):
    return [perm(block, route(i)) for i, block in enumerate(blocks, start=first)]


def gathered(own):
    mine = [own] + shifted([own] * (NX - 1), along_x)
    stack = stacked(mine)
    return mine + [perm(stack, partner)]


def local(panel, diag_tiles, dinv, u_fac, v_fac, ranks, sketch):
    panel, dinv = panel[0], dinv[0]
    u, v, ranks = u_fac[0, :, 0], v_fac[0, :, 0], ranks[0, :, 0]
    small = sketch.shape[1:]
    split = [((NX,) + small, BF16), ((NX,) + small, F32)]

    send, keep = sketch_call(ranks, v, u, sketch[0])
    got = perm(send, partner)
    panel_send, panel_keep = split_panel(panel)
    panel_got = perm(panel_send, partner)
    own, *others = pair_sum(keep, got)
    others = shifted(others, along_x)
    panel_bundles = bundles(panel_keep, panel_got, 1)
    rows = [panel_keep, panel_got] + shifted(panel_bundles, along_x)
    own_sum = owner_total(own, others)
    sums = gathered(own_sum)
    inverse = gram_inverse(own_sum)
    send, keep = sum_product(split, ranks, u, v, sums)
    got = perm(send, partner)
    own, *others = pair_sum(keep, got)
    others = shifted(others, along_x)
    tile = tile_call(own_sum, inverse, [own, *others], dinv, rows)
    cross, *blocks = tile
    arrived = [None] * NU
    for i in ORDER:
        arrived[i] = perm(blocks[i], to_column(i // 2, i % 2))
    crosses = gathered(cross)
    here, onward = arrived_sum(arrived)
    onward = [perm(onward, along_z(1))]
    total, *mirrored = collect(here, onward)
    mirrored = shifted(mirrored, lambda d: along_upd(-d))
    panel_out = rows_call(panel, dinv, sums, crosses)
    diag_out = diag_call(diag_tiles[0], total, mirrored)
    return (panel_out[None], diag_out[None])


ORDER = (2, 6, 3, 7, 4, 5, 0, 1)


def solution(mesh):
    in_specs = (
        P("col", None, "upd", None),
        P("col", "upd", None),
        P("col", None, None),
        P("col", None, "upd", None, None),
        P("col", None, "upd", None, None),
        P("col", None, "upd"),
        P("col", None, None),
    )
    out_specs = (P("col", None, "upd", None), P("col", "upd", None))
    return jax.shard_map(local, mesh=mesh, in_specs=in_specs, out_specs=out_specs, check_vma=False)
```

profile of v0, /device:TPU:1, one launch (start us, length us, event | category | flops | bytes accessed | tf_op | source)
XLA Modules:
  0.0 138.8 jit_solution(10452296449707945503)
XLA Ops:
  1.4 5.4 %sketch_product.1 = (bf16[4,64,1024]{2,1,0:T(8,128)(2,1)S(1)}, f32[4,64,1024]{2,1,0:T(8,128)S(1)}) custom-call(s32[8]{0:T(128)S(1)} %bitcast.18, bf16[8,96,1024]{2,1,0:T(8,128)(2,1)} %bitcast.13, bf16[8,96,1024]{2,1,0:T(8,128)(2,1)} %bitcast.15, bf16[64,1024]{1,0:T(8,128)(2,1)} %bitcast.22), custom_call_target="tpu_custom_call" | custom-call | tf_op jit(solution)/shard_map/sketch_product/pallas_call | solution.py:121
  6.9 3.3 %collective-permute-start = (bf16[4,64,1024]{2,1,0:T(8,128)(2,1)S(1)}, bf16[4,64,1024]{2,1,0:T(8,128)(2,1)S(1)}, u32[]{:S(2)}, u32[]{:S(2)}) collective-permute-start(bf16[4,64,1024]{2,1,0:T(8,128)(2,1)S(1)} %get-tuple-element.35), channel_id=1, source_target_pairs={{0,32},{1,33},{2,34},{3,35},{4,36},{5,37},{6,38},{7,39},{8,40},{9,... | collective-permute-start | bytes 1572872 | tf_op jit(solution)/shard_map/ppermute | solution.py:40
  10.5 1.2 collective-permute-done.got_ref
  11.9 1.9 %collective-permute-start.2 = (bf16[64,1024]{1,0:T(8,128)(2,1)S(1)}, bf16[64,1024]{1,0:T(8,128)(2,1)S(1)}, u32[]{:S(2)}, u32[]{:S(2)}) collective-permute-start(bf16[64,1024]{1,0:T(8,128)(2,1)S(1)} %get-tuple-element.38), channel_id=1, source_target_pairs={{0,128},{1,129},{2,130},{3,131},{4,132},{5,133},{6,134},{7,135},{8... | collective-permute-start | bytes 393224 | tf_op jit(solution)/shard_map/ppermute | solution.py:40
  13.9 1.2 collective-permute-start.3
  15.0 3.5 %collective-permute-done.1.a_ref = bf16[64,1024]{1,0:T(8,128)(2,1)S(1)} collective-permute-done((bf16[64,1024]{1,0:T(8,128)(2,1)S(1)}, bf16[64,1024]{1,0:T(8,128)(2,1)S(1)}, u32[]{:S(2)}, u32[]{:S(2)}) %collective-permute-start.1) | collective-permute-done | bytes 131104 | tf_op jit(solution)/shard_map/ppermute | solution.py:40
  18.5 1.4 %collective-permute-done.2.b_ref = bf16[64,1024]{1,0:T(8,128)(2,1)S(1)} collective-permute-done((bf16[64,1024]{1,0:T(8,128)(2,1)S(1)}, bf16[64,1024]{1,0:T(8,128)(2,1)S(1)}, u32[]{:S(2)}, u32[]{:S(2)}) %collective-permute-start.2) | collective-permute-done | bytes 131104 | tf_op jit(solution)/shard_map/ppermute | solution.py:40
  21.0 3.5 %collective-permute-start.6 = (bf16[64,1024]{1,0:T(8,128)(2,1)S(1)}, bf16[64,1024]{1,0:T(8,128)(2,1)S(1)}, u32[]{:S(2)}, u32[]{:S(2)}) collective-permute-start(bf16[64,1024]{1,0:T(8,128)(2,1)S(1)} %shard_map.87.a_ref.summed_ref.refs_0_.sum_ref), channel_id=1, source_target_pairs={{0,192},{1,193},{2,194},{3,195},{4,196},{5,197},{6,198},{7,199},{8... | collective-permute-start | bytes 393224 | tf_op jit(solution)/shard_map/ppermute | solution.py:40
  25.1 4.6 %collective-permute-done.6.d_ref.refs_3_ = bf16[64,1024]{1,0:T(8,128)(2,1)S(1)} collective-permute-done((bf16[64,1024]{1,0:T(8,128)(2,1)S(1)}, bf16[64,1024]{1,0:T(8,128)(2,1)S(1)}, u32[]{:S(2)}, u32[]{:S(2)}) %collective-permute-start.6) | collective-permute-done | bytes 131104 | tf_op jit(solution)/shard_map/ppermute | solution.py:40
  30.3 3.3 %collective-permute-done.4.b_ref.refs_1_ = bf16[64,1024]{1,0:T(8,128)(2,1)S(1)} collective-permute-done((bf16[64,1024]{1,0:T(8,128)(2,1)S(1)}, bf16[64,1024]{1,0:T(8,128)(2,1)S(1)}, u32[]{:S(2)}, u32[]{:S(2)}) %collective-permute-start.4) | collective-permute-done | bytes 131104 | tf_op jit(solution)/shard_map/ppermute | solution.py:40
  34.5 1.5 %collective-permute-done.7.refs_4_ = bf16[4,64,1024]{2,1,0:T(8,128)(2,1)S(1)} collective-permute-done((bf16[4,64,1024]{2,1,0:T(8,128)(2,1)S(1)}, bf16[4,64,1024]{2,1,0:T(8,128)(2,1)S(1)}, u32[]{:S(2)}, u32[]{:S(2)}) %collective-permute-start.7) | collective-permute-done | bytes 524320 | tf_op jit(solution)/shard_map/ppermute | solution.py:40
  36.1 3.1 %shard_map.90 = (bf16[4,64,1024]{2,1,0:T(8,128)(2,1)S(1)}, f32[4,64,1024]{2,1,0:T(8,128)S(1)}) custom-call(s32[8]{0:T(128)S(1)} %bitcast.19, bf16[8,96,1024]{2,1,0:T(8,128)(2,1)S(1)} %bitcast.16, bf16[8,96,1024]{2,1,0:T(8,128)(2,1)S(1)} %bitcast.14, bf16[64,1024]{1,0:T(8,128)(2,1)S(1)} %shard_map.87.a_ref.summed_ref.refs_0_.sum_ref, ...), custom_call_target="tpu_custom_call" | custom-call | tf_op jit(solution)/shard_map/pallas_call | solution.py:75
  39.8 1.8 %collective-permute-start.14 = (bf16[2,128,1024]{2,1,0:T(8,128)(2,1)S(1)}, bf16[2,128,1024]{2,1,0:T(8,128)(2,1)S(1)}, u32[]{:S(2)}, u32[]{:S(2)}) collective-permute-start(bf16[2,128,1024]{2,1,0:T(8,128)(2,1)S(1)} %get-tuple-element.49), channel_id=1, source_target_pairs={{0,128},{1,129},{2,130},{3,131},{4,132},{5,133},{6,134},{7,135},{8... | collective-permute-start | bytes 1572872 | tf_op jit(solution)/shard_map/ppermute | solution.py:40
  43.4 1.9 %collective-permute-start.10 = (bf16[64,1024]{1,0:T(8,128)(2,1)S(1)}, bf16[64,1024]{1,0:T(8,128)(2,1)S(1)}, u32[]{:S(2)}, u32[]{:S(2)}) collective-permute-start(bf16[64,1024]{1,0:T(8,128)(2,1)S(1)} %get-tuple-element.44), channel_id=1, source_target_pairs={{0,128},{1,129},{2,130},{3,131},{4,132},{5,133},{6,134},{7,135},{8... | collective-permute-start | bytes 393224 | tf_op jit(solution)/shard_map/ppermute | solution.py:40
  45.3 19.9 %collective-permute-done.13.refs_2_ = bf16[2,128,1024]{2,1,0:T(8,128)(2,1)S(1)} collective-permute-done((bf16[2,128,1024]{2,1,0:T(8,128)(2,1)S(1)}, bf16[2,128,1024]{2,1,0:T(8,128)(2,1)S(1)}, u32[]{:S(2)}, u32[]{:S(2)}) %collective-permute-start.13) | collective-permute-done | bytes 524320 | tf_op jit(solution)/shard_map/ppermute | solution.py:40
  65.2 6.1 %shard_map.89.inverse_ref = f32[64,64]{1,0:T(8,128)S(1)} custom-call(bf16[64,1024]{1,0:T(8,128)(2,1)S(1)} %shard_map.87.a_ref.summed_ref.refs_0_.sum_ref), custom_call_target="tpu_custom_call" | custom-call | tf_op jit(solution)/shard_map/pallas_call | solution.py:75
  71.6 5.6 %shard_map.94 = (bf16[64,1024]{1,0:T(8,128)(2,1)S(1)}, bf16[128,640]{1,0:T(8,128)(2,1)S(1)}, bf16[128,640]{1,0:T(8,128)(2,1)S(1)}, bf16[128,640]{1,0:T(8,128)(2,...) custom-call(bf16[64,1024]{1,0:T(8,128)(2,1)S(1)} %shard_map.87.a_ref, ...), custom_call_target="tpu_custom_call" | custom-call | tf_op jit(solution)/shard_map/pallas_call | solution.py:75
  77.2 2.5 %collective-permute-start.18 = (bf16[64,1024]{1,0:T(8,128)(2,1)S(1)}, bf16[64,1024]{1,0:T(8,128)(2,1)S(1)}, u32[]{:S(2)}, u32[]{:S(2)}) collective-permute-start(bf16[64,1024]{1,0:T(8,128)(2,1)S(1)} %get-tuple-element.51.a_ref.refs_5_), channel_id=1, source_target_pairs={{0,192},{1,193},{2,194},{3,195},{4,196},{5,197},{6,198},{7,199},{8... | collective-permute-start | bytes 393224 | tf_op jit(solution)/shard_map/ppermute | solution.py:40
  80.4 2.9 %collective-permute-start.20 = (bf16[128,640]{1,0:T(8,128)(2,1)S(1)}, bf16[128,640]{1,0:T(8,128)(2,1)S(1)}, u32[]{:S(2)}, u32[]{:S(2)}) collective-permute-start(bf16[128,640]{1,0:T(8,128)(2,1)S(1)} %get-tuple-element.52), channel_id=1, source_target_pairs={{0,1},{1,2},{2,3},{3,0},{4,5},{5,6},{6,7},{7,4},{8,9},{9,10},{10,1... | collective-permute-start | bytes 491528 | tf_op jit(solution)/shard_map/ppermute | solution.py:40
  83.3 3.9 %collective-permute-start.21 = (bf16[128,640]{1,0:T(8,128)(2,1)S(1)}, bf16[128,640]{1,0:T(8,128)(2,1)S(1)}, u32[]{:S(2)}, u32[]{:S(2)}) collective-permute-start(bf16[128,640]{1,0:T(8,128)(2,1)S(1)} %get-tuple-element.53), channel_id=1, source_target_pairs={{0,33},{1,34},{2,35},{3,32},{4,37},{5,38},{6,39},{7,36},{8,41},{9,... | collective-permute-start | bytes 491528 | tf_op jit(solution)/shard_map/ppermute | solution.py:40
  87.2 3.9 %collective-permute-start.22 = (bf16[128,640]{1,0:T(8,128)(2,1)S(1)}, bf16[128,640]{1,0:T(8,128)(2,1)S(1)}, u32[]{:S(2)}, u32[]{:S(2)}) collective-permute-start(bf16[128,640]{1,0:T(8,128)(2,1)S(1)} %get-tuple-element.54), channel_id=1, source_target_pairs={{0,65},{1,66},{2,67},{3,64},{4,69},{5,70},{6,71},{7,68},{8,73},{9,... | collective-permute-start | bytes 491528 | tf_op jit(solution)/shard_map/ppermute | solution.py:40
  91.5 3.7 %collective-permute-start.24 = (bf16[128,640]{1,0:T(8,128)(2,1)S(1)}, bf16[128,640]{1,0:T(8,128)(2,1)S(1)}, u32[]{:S(2)}, u32[]{:S(2)}) collective-permute-start(bf16[128,640]{1,0:T(8,128)(2,1)S(1)} %get-tuple-element.56), channel_id=1, source_target_pairs={{0,129},{1,130},{2,131},{3,128},{4,133},{5,134},{6,135},{7,132},{8... | collective-permute-start | bytes 491528 | tf_op jit(solution)/shard_map/ppermute | solution.py:40
  95.2 1.2 collective-permute-done.21.refs_1_
  96.4 4.6 %collective-permute-start.25 = (bf16[128,640]{1,0:T(8,128)(2,1)S(1)}, bf16[128,640]{1,0:T(8,128)(2,1)S(1)}, u32[]{:S(2)}, u32[]{:S(2)}) collective-permute-start(bf16[128,640]{1,0:T(8,128)(2,1)S(1)} %get-tuple-element.57), channel_id=1, source_target_pairs={{0,161},{1,162},{2,163},{3,160},{4,165},{5,166},{6,167},{7,164},{8... | collective-permute-start | bytes 491528 | tf_op jit(solution)/shard_map/ppermute | solution.py:40
  101.0 1.8 %collective-permute-start.26 = (bf16[128,640]{1,0:T(8,128)(2,1)S(1)}, bf16[128,640]{1,0:T(8,128)(2,1)S(1)}, u32[]{:S(2)}, u32[]{:S(2)}) collective-permute-start(bf16[128,640]{1,0:T(8,128)(2,1)S(1)} %get-tuple-element.58), channel_id=1, source_target_pairs={{0,193},{1,194},{2,195},{3,192},{4,197},{5,198},{6,199},{7,196},{8... | collective-permute-start | bytes 491528 | tf_op jit(solution)/shard_map/ppermute | solution.py:40
  102.9 3.4 %collective-permute-done.25.refs_5_ = bf16[128,640]{1,0:T(8,128)(2,1)S(1)} collective-permute-done((bf16[128,640]{1,0:T(8,128)(2,1)S(1)}, bf16[128,640]{1,0:T(8,128)(2,1)S(1)}, u32[]{:S(2)}, u32[]{:S(2)}) %collective-permute-start.25) | collective-permute-done | bytes 163872 | tf_op jit(solution)/shard_map/ppermute | solution.py:40
  106.4 8.6 %collective-permute-done.26.refs_6_ = bf16[128,640]{1,0:T(8,128)(2,1)S(1)} collective-permute-done((bf16[128,640]{1,0:T(8,128)(2,1)S(1)}, bf16[128,640]{1,0:T(8,128)(2,1)S(1)}, u32[]{:S(2)}, u32[]{:S(2)}) %collective-permute-start.26) | collective-permute-done | bytes 163872 | tf_op jit(solution)/shard_map/ppermute | solution.py:40
  115.4 2.3 %collective-permute-start.28 = (bf16[128,640]{1,0:T(8,128)(2,1)S(1)}, bf16[128,640]{1,0:T(8,128)(2,1)S(1)}, u32[]{:S(2)}, u32[]{:S(2)}) collective-permute-start(bf16[128,640]{1,0:T(8,128)(2,1)S(1)} %get-tuple-element.61), channel_id=1, source_target_pairs={{0,4},{1,5},{2,6},{3,7},{4,8},{5,9},{6,10},{7,11},{8,12},{9,13},{1... | collective-permute-start | bytes 491528 | tf_op jit(solution)/shard_map/ppermute | solution.py:40
  117.6 6.9 %collective-permute-done.28.onward_ref = bf16[128,640]{1,0:T(8,128)(2,1)S(1)} collective-permute-done((bf16[128,640]{1,0:T(8,128)(2,1)S(1)}, bf16[128,640]{1,0:T(8,128)(2,1)S(1)}, u32[]{:S(2)}, u32[]{:S(2)}) %collective-permute-start.28) | collective-permute-done | bytes 163872 | tf_op jit(solution)/shard_map/ppermute | solution.py:40
  125.7 3.2 %collective-permute-start.30 = (bf16[128,128]{1,0:T(8,128)(2,1)S(1)}, bf16[128,128]{1,0:T(8,128)(2,1)S(1)}, u32[]{:S(2)}, u32[]{:S(2)}) collective-permute-start(bf16[128,128]{1,0:T(8,128)(2,1)S(1)} %get-tuple-element.64), channel_id=1, source_target_pairs={{0,192},{1,193},{2,194},{3,195},{4,196},{5,197},{6,198},{7,199},{8... | collective-permute-start | bytes 98312 | tf_op jit(solution)/shard_map/ppermute | solution.py:40
  129.9 3.8 %collective-permute-done.31.c_ref = bf16[128,128]{1,0:T(8,128)(2,1)S(1)} collective-permute-done((bf16[128,128]{1,0:T(8,128)(2,1)S(1)}, bf16[128,128]{1,0:T(8,128)(2,1)S(1)}, u32[]{:S(2)}, u32[]{:S(2)}) %collective-permute-start.31) | collective-permute-done | bytes 32800 | tf_op jit(solution)/shard_map/ppermute | solution.py:40
  134.6 4.0 %shard_map.96 = bf16[8,128,1024]{2,1,0:T(8,128)(2,1)} custom-call(bf16[8,128,1024]{2,1,0:T(8,128)(2,1)S(1)} %bitcast.12, bf16[1024,1024]{1,0:T(8,128)(2,1)S(1)} %bitcast.10, bf16[64,1024]{1,0:T(8,128)(2,1)S(1)} %shard_map.87.a_ref.summed_ref.refs_0_.sum_ref, bf16[64,1024]{1,0:T(8,128)(2,1)S(1)} %collective-permute-done.4.b_ref.refs_1_, ...), custom_call_target="tpu_custom_call" | custom-call | tf_op jit(solution)/shard_map/pallas_call | solution.py:75
  (61 shorter events, 11.9 us)
Async XLA Ops:
  6.9 4.8 %collective-permute-start = (bf16[4,64,1024]{2,1,0:T(8,128)(2,1)S(1)}, bf16[4,64,1024]{2,1,0:T(8,128)(2,1)S(1)}, u32[]{:S(2)}, u32[]{:S(2)}) collective-permute-start(bf16[4,64,1024]{2,1,0:T(8,128)(2,1)S(1)} %get-tuple-element.35), channel_id=1, source_target_pairs={{0,32},{1,33},{2,34},{3,35},{4,36},{5,37},{6,38},{7,39},{8,40},{9,... | collective-permute-start | bytes 1572872 | tf_op jit(solution)/shard_map/ppermute | solution.py:40
  10.4 29.3 %collective-permute-start.12 = (bf16[4,128,1024]{2,1,0:T(8,128)(2,1)S(1)}, bf16[4,128,1024]{2,1,0:T(8,128)(2,1)S(1)}, u32[]{:S(2)}, u32[]{:S(2)}) collective-permute-start(bf16[4,128,1024]{2,1,0:T(8,128)(2,1)S(1)} %get-tuple-element.47), channel_id=1, source_target_pairs={{0,32},{1,33},{2,34},{3,35},{4,36},{5,37},{6,38},{7,39},{8,40},{9,... | collective-permute-start | bytes 3145736 | tf_op jit(solution)/shard_map/ppermute | solution.py:40
  11.8 6.7 %collective-permute-start.1 = (bf16[64,1024]{1,0:T(8,128)(2,1)S(1)}, bf16[64,1024]{1,0:T(8,128)(2,1)S(1)}, u32[]{:S(2)}, u32[]{:S(2)}) collective-permute-start(bf16[64,1024]{1,0:T(8,128)(2,1)S(1)} %get-tuple-element.37), channel_id=1, source_target_pairs={{0,64},{1,65},{2,66},{3,67},{4,68},{5,69},{6,70},{7,71},{8,72},{9,... | collective-permute-start | bytes 393224 | tf_op jit(solution)/shard_map/ppermute | solution.py:40
  11.9 8.0 %collective-permute-start.2 = (bf16[64,1024]{1,0:T(8,128)(2,1)S(1)}, bf16[64,1024]{1,0:T(8,128)(2,1)S(1)}, u32[]{:S(2)}, u32[]{:S(2)}) collective-permute-start(bf16[64,1024]{1,0:T(8,128)(2,1)S(1)} %get-tuple-element.38), channel_id=1, source_target_pairs={{0,128},{1,129},{2,130},{3,131},{4,132},{5,133},{6,134},{7,135},{8... | collective-permute-start | bytes 393224 | tf_op jit(solution)/shard_map/ppermute | solution.py:40
  13.9 7.0 %collective-permute-start.3 = (bf16[64,1024]{1,0:T(8,128)(2,1)S(1)}, bf16[64,1024]{1,0:T(8,128)(2,1)S(1)}, u32[]{:S(2)}, u32[]{:S(2)}) collective-permute-start(bf16[64,1024]{1,0:T(8,128)(2,1)S(1)} %get-tuple-element.39), channel_id=1, source_target_pairs={{0,192},{1,193},{2,194},{3,195},{4,196},{5,197},{6,198},{7,199},{8... | collective-permute-start | bytes 393224 | tf_op jit(solution)/shard_map/ppermute | solution.py:40
  21.0 8.8 %collective-permute-start.6 = (bf16[64,1024]{1,0:T(8,128)(2,1)S(1)}, bf16[64,1024]{1,0:T(8,128)(2,1)S(1)}, u32[]{:S(2)}, u32[]{:S(2)}) collective-permute-start(bf16[64,1024]{1,0:T(8,128)(2,1)S(1)} %shard_map.87.a_ref.summed_ref.refs_0_.sum_ref), channel_id=1, source_target_pairs={{0,192},{1,193},{2,194},{3,195},{4,196},{5,197},{6,198},{7,199},{8... | collective-permute-start | bytes 393224 | tf_op jit(solution)/shard_map/ppermute | solution.py:40
  24.5 5.9 %collective-permute-start.5 = (bf16[64,1024]{1,0:T(8,128)(2,1)S(1)}, bf16[64,1024]{1,0:T(8,128)(2,1)S(1)}, u32[]{:S(2)}, u32[]{:S(2)}) collective-permute-start(bf16[64,1024]{1,0:T(8,128)(2,1)S(1)} %shard_map.87.a_ref.summed_ref.refs_0_.sum_ref), channel_id=1, source_target_pairs={{0,128},{1,129},{2,130},{3,131},{4,132},{5,133},{6,134},{7,135},{8... | collective-permute-start | bytes 393224 | tf_op jit(solution)/shard_map/ppermute | solution.py:40
  24.5 9.1 %collective-permute-start.4 = (bf16[64,1024]{1,0:T(8,128)(2,1)S(1)}, bf16[64,1024]{1,0:T(8,128)(2,1)S(1)}, u32[]{:S(2)}, u32[]{:S(2)}) collective-permute-start(bf16[64,1024]{1,0:T(8,128)(2,1)S(1)} %shard_map.87.a_ref.summed_ref.refs_0_.sum_ref), channel_id=1, source_target_pairs={{0,64},{1,65},{2,66},{3,67},{4,68},{5,69},{6,70},{7,71},{8,72},{9,... | collective-permute-start | bytes 393224 | tf_op jit(solution)/shard_map/ppermute | solution.py:40
  33.6 2.4 %collective-permute-start.7 = (bf16[4,64,1024]{2,1,0:T(8,128)(2,1)S(1)}, bf16[4,64,1024]{2,1,0:T(8,128)(2,1)S(1)}, u32[]{:S(2)}, u32[]{:S(2)}) collective-permute-start(bf16[4,64,1024]{2,1,0:T(8,128)(2,1)S(1)} %shard_map.88), channel_id=1, source_target_pairs={{0,32},{1,33},{2,34},{3,35},{4,36},{5,37},{6,38},{7,39},{8,40},{9,... | collective-permute-start | bytes 1572872 | tf_op jit(solution)/shard_map/ppermute | solution.py:40
  39.2 3.3 %collective-permute-start.8 = (bf16[4,64,1024]{2,1,0:T(8,128)(2,1)S(1)}, bf16[4,64,1024]{2,1,0:T(8,128)(2,1)S(1)}, u32[]{:S(2)}, u32[]{:S(2)}) collective-permute-start(bf16[4,64,1024]{2,1,0:T(8,128)(2,1)S(1)} %get-tuple-element.41), channel_id=1, source_target_pairs={{0,32},{1,33},{2,34},{3,35},{4,36},{5,37},{6,38},{7,39},{8,40},{9,... | collective-permute-start | bytes 1572872 | tf_op jit(solution)/shard_map/ppermute | solution.py:40
  39.7 25.5 %collective-permute-start.13 = (bf16[2,128,1024]{2,1,0:T(8,128)(2,1)S(1)}, bf16[2,128,1024]{2,1,0:T(8,128)(2,1)S(1)}, u32[]{:S(2)}, u32[]{:S(2)}) collective-permute-start(bf16[2,128,1024]{2,1,0:T(8,128)(2,1)S(1)} %get-tuple-element.48), channel_id=1, source_target_pairs={{0,64},{1,65},{2,66},{3,67},{4,68},{5,69},{6,70},{7,71},{8,72},{9,... | collective-permute-start | bytes 1572872 | tf_op jit(solution)/shard_map/ppermute | solution.py:40
  39.8 31.5 %collective-permute-start.14 = (bf16[2,128,1024]{2,1,0:T(8,128)(2,1)S(1)}, bf16[2,128,1024]{2,1,0:T(8,128)(2,1)S(1)}, u32[]{:S(2)}, u32[]{:S(2)}) collective-permute-start(bf16[2,128,1024]{2,1,0:T(8,128)(2,1)S(1)} %get-tuple-element.49), channel_id=1, source_target_pairs={{0,128},{1,129},{2,130},{3,131},{4,132},{5,133},{6,134},{7,135},{8... | collective-permute-start | bytes 1572872 | tf_op jit(solution)/shard_map/ppermute | solution.py:40
  41.6 29.7 %collective-permute-start.15 = (bf16[2,128,1024]{2,1,0:T(8,128)(2,1)S(1)}, bf16[2,128,1024]{2,1,0:T(8,128)(2,1)S(1)}, u32[]{:S(2)}, u32[]{:S(2)}) collective-permute-start(bf16[2,128,1024]{2,1,0:T(8,128)(2,1)S(1)} %get-tuple-element.50), channel_id=1, source_target_pairs={{0,192},{1,193},{2,194},{3,195},{4,196},{5,197},{6,198},{7,199},{8... | collective-permute-start | bytes 1572872 | tf_op jit(solution)/shard_map/ppermute | solution.py:40
  42.6 28.8 %collective-permute-start.9 = (bf16[64,1024]{1,0:T(8,128)(2,1)S(1)}, bf16[64,1024]{1,0:T(8,128)(2,1)S(1)}, u32[]{:S(2)}, u32[]{:S(2)}) collective-permute-start(bf16[64,1024]{1,0:T(8,128)(2,1)S(1)} %get-tuple-element.43), channel_id=1, source_target_pairs={{0,64},{1,65},{2,66},{3,67},{4,68},{5,69},{6,70},{7,71},{8,72},{9,... | collective-permute-start | bytes 393224 | tf_op jit(solution)/shard_map/ppermute | solution.py:40
  43.4 27.9 %collective-permute-start.10 = (bf16[64,1024]{1,0:T(8,128)(2,1)S(1)}, bf16[64,1024]{1,0:T(8,128)(2,1)S(1)}, u32[]{:S(2)}, u32[]{:S(2)}) collective-permute-start(bf16[64,1024]{1,0:T(8,128)(2,1)S(1)} %get-tuple-element.44), channel_id=1, source_target_pairs={{0,128},{1,129},{2,130},{3,131},{4,132},{5,133},{6,134},{7,135},{8... | collective-permute-start | bytes 393224 | tf_op jit(solution)/shard_map/ppermute | solution.py:40
  65.2 6.4 %collective-permute-start.11 = (bf16[64,1024]{1,0:T(8,128)(2,1)S(1)}, bf16[64,1024]{1,0:T(8,128)(2,1)S(1)}, u32[]{:S(2)}, u32[]{:S(2)}) collective-permute-start(bf16[64,1024]{1,0:T(8,128)(2,1)S(1)} %get-tuple-element.45), channel_id=1, source_target_pairs={{0,192},{1,193},{2,194},{3,195},{4,196},{5,197},{6,198},{7,199},{8... | collective-permute-start | bytes 393224 | tf_op jit(solution)/shard_map/ppermute | solution.py:40
  77.2 10.0 %collective-permute-start.18 = (bf16[64,1024]{1,0:T(8,128)(2,1)S(1)}, bf16[64,1024]{1,0:T(8,128)(2,1)S(1)}, u32[]{:S(2)}, u32[]{:S(2)}) collective-permute-start(bf16[64,1024]{1,0:T(8,128)(2,1)S(1)} %get-tuple-element.51.a_ref.refs_5_), channel_id=1, source_target_pairs={{0,192},{1,193},{2,194},{3,195},{4,196},{5,197},{6,198},{7,199},{8... | collective-permute-start | bytes 393224 | tf_op jit(solution)/shard_map/ppermute | solution.py:40
  79.8 11.3 %collective-permute-start.17 = (bf16[64,1024]{1,0:T(8,128)(2,1)S(1)}, bf16[64,1024]{1,0:T(8,128)(2,1)S(1)}, u32[]{:S(2)}, u32[]{:S(2)}) collective-permute-start(bf16[64,1024]{1,0:T(8,128)(2,1)S(1)} %get-tuple-element.51.a_ref.refs_5_), channel_id=1, source_target_pairs={{0,128},{1,129},{2,130},{3,131},{4,132},{5,133},{6,134},{7,135},{8... | collective-permute-start | bytes 393224 | tf_op jit(solution)/shard_map/ppermute | solution.py:40
  80.4 10.7 %collective-permute-start.16 = (bf16[64,1024]{1,0:T(8,128)(2,1)S(1)}, bf16[64,1024]{1,0:T(8,128)(2,1)S(1)}, u32[]{:S(2)}, u32[]{:S(2)}) collective-permute-start(bf16[64,1024]{1,0:T(8,128)(2,1)S(1)} %get-tuple-element.51.a_ref.refs_5_), channel_id=1, source_target_pairs={{0,64},{1,65},{2,66},{3,67},{4,68},{5,69},{6,70},{7,71},{8,72},{9,... | collective-permute-start | bytes 393224 | tf_op jit(solution)/shard_map/ppermute | solution.py:40
  80.4 11.0 %collective-permute-start.20 = (bf16[128,640]{1,0:T(8,128)(2,1)S(1)}, bf16[128,640]{1,0:T(8,128)(2,1)S(1)}, u32[]{:S(2)}, u32[]{:S(2)}) collective-permute-start(bf16[128,640]{1,0:T(8,128)(2,1)S(1)} %get-tuple-element.52), channel_id=1, source_target_pairs={{0,1},{1,2},{2,3},{3,0},{4,5},{5,6},{6,7},{7,4},{8,9},{9,10},{10,1... | collective-permute-start | bytes 491528 | tf_op jit(solution)/shard_map/ppermute | solution.py:40
  83.3 13.1 %collective-permute-start.21 = (bf16[128,640]{1,0:T(8,128)(2,1)S(1)}, bf16[128,640]{1,0:T(8,128)(2,1)S(1)}, u32[]{:S(2)}, u32[]{:S(2)}) collective-permute-start(bf16[128,640]{1,0:T(8,128)(2,1)S(1)} %get-tuple-element.53), channel_id=1, source_target_pairs={{0,33},{1,34},{2,35},{3,32},{4,37},{5,38},{6,39},{7,36},{8,41},{9,... | collective-permute-start | bytes 491528 | tf_op jit(solution)/shard_map/ppermute | solution.py:40
  87.2 13.8 %collective-permute-start.22 = (bf16[128,640]{1,0:T(8,128)(2,1)S(1)}, bf16[128,640]{1,0:T(8,128)(2,1)S(1)}, u32[]{:S(2)}, u32[]{:S(2)}) collective-permute-start(bf16[128,640]{1,0:T(8,128)(2,1)S(1)} %get-tuple-element.54), channel_id=1, source_target_pairs={{0,65},{1,66},{2,67},{3,64},{4,69},{5,70},{6,71},{7,68},{8,73},{9,... | collective-permute-start | bytes 491528 | tf_op jit(solution)/shard_map/ppermute | solution.py:40
  91.1 11.8 %collective-permute-start.23 = (bf16[128,640]{1,0:T(8,128)(2,1)S(1)}, bf16[128,640]{1,0:T(8,128)(2,1)S(1)}, u32[]{:S(2)}, u32[]{:S(2)}) collective-permute-start(bf16[128,640]{1,0:T(8,128)(2,1)S(1)} %get-tuple-element.55), channel_id=1, source_target_pairs={{0,97},{1,98},{2,99},{3,96},{4,101},{5,102},{6,103},{7,100},{8,105... | collective-permute-start | bytes 491528 | tf_op jit(solution)/shard_map/ppermute | solution.py:40
  91.1 43.5 %collective-permute-start.19 = (bf16[4,64,1024]{2,1,0:T(8,128)(2,1)S(1)}, bf16[4,64,1024]{2,1,0:T(8,128)(2,1)S(1)}, u32[]{:S(2)}, u32[]{:S(2)}) collective-permute-start(bf16[4,64,1024]{2,1,0:T(8,128)(2,1)S(1)} %shard_map.95), channel_id=1, source_target_pairs={{0,32},{1,33},{2,34},{3,35},{4,36},{5,37},{6,38},{7,39},{8,40},{9,... | collective-permute-start | bytes 1572872 | tf_op jit(solution)/shard_map/ppermute | solution.py:40
  91.5 11.5 %collective-permute-start.24 = (bf16[128,640]{1,0:T(8,128)(2,1)S(1)}, bf16[128,640]{1,0:T(8,128)(2,1)S(1)}, u32[]{:S(2)}, u32[]{:S(2)}) collective-permute-start(bf16[128,640]{1,0:T(8,128)(2,1)S(1)} %get-tuple-element.56), channel_id=1, source_target_pairs={{0,129},{1,130},{2,131},{3,128},{4,133},{5,134},{6,135},{7,132},{8... | collective-permute-start | bytes 491528 | tf_op jit(solution)/shard_map/ppermute | solution.py:40
  96.4 10.0 %collective-permute-start.25 = (bf16[128,640]{1,0:T(8,128)(2,1)S(1)}, bf16[128,640]{1,0:T(8,128)(2,1)S(1)}, u32[]{:S(2)}, u32[]{:S(2)}) collective-permute-start(bf16[128,640]{1,0:T(8,128)(2,1)S(1)} %get-tuple-element.57), channel_id=1, source_target_pairs={{0,161},{1,162},{2,163},{3,160},{4,165},{5,166},{6,167},{7,164},{8... | collective-permute-start | bytes 491528 | tf_op jit(solution)/shard_map/ppermute | solution.py:40
  101.0 13.9 %collective-permute-start.26 = (bf16[128,640]{1,0:T(8,128)(2,1)S(1)}, bf16[128,640]{1,0:T(8,128)(2,1)S(1)}, u32[]{:S(2)}, u32[]{:S(2)}) collective-permute-start(bf16[128,640]{1,0:T(8,128)(2,1)S(1)} %get-tuple-element.58), channel_id=1, source_target_pairs={{0,193},{1,194},{2,195},{3,192},{4,197},{5,198},{6,199},{7,196},{8... | collective-permute-start | bytes 491528 | tf_op jit(solution)/shard_map/ppermute | solution.py:40
  102.8 12.1 %collective-permute-start.27 = (bf16[128,640]{1,0:T(8,128)(2,1)S(1)}, bf16[128,640]{1,0:T(8,128)(2,1)S(1)}, u32[]{:S(2)}, u32[]{:S(2)}) collective-permute-start(bf16[128,640]{1,0:T(8,128)(2,1)S(1)} %get-tuple-element.59), channel_id=1, source_target_pairs={{0,225},{1,226},{2,227},{3,224},{4,229},{5,230},{6,231},{7,228},{8... | collective-permute-start | bytes 491528 | tf_op jit(solution)/shard_map/ppermute | solution.py:40
  115.4 9.1 %collective-permute-start.28 = (bf16[128,640]{1,0:T(8,128)(2,1)S(1)}, bf16[128,640]{1,0:T(8,128)(2,1)S(1)}, u32[]{:S(2)}, u32[]{:S(2)}) collective-permute-start(bf16[128,640]{1,0:T(8,128)(2,1)S(1)} %get-tuple-element.61), channel_id=1, source_target_pairs={{0,4},{1,5},{2,6},{3,7},{4,8},{5,9},{6,10},{7,11},{8,12},{9,13},{1... | collective-permute-start | bytes 491528 | tf_op jit(solution)/shard_map/ppermute | solution.py:40
  124.6 4.3 %collective-permute-start.29 = (bf16[128,128]{1,0:T(8,128)(2,1)S(1)}, bf16[128,128]{1,0:T(8,128)(2,1)S(1)}, u32[]{:S(2)}, u32[]{:S(2)}) collective-permute-start(bf16[128,128]{1,0:T(8,128)(2,1)S(1)} %get-tuple-element.63), channel_id=1, source_target_pairs={{0,224},{1,225},{2,226},{3,227},{4,228},{5,229},{6,230},{7,231},{8... | collective-permute-start | bytes 98312 | tf_op jit(solution)/shard_map/ppermute | solution.py:40
  125.7 4.3 %collective-permute-start.30 = (bf16[128,128]{1,0:T(8,128)(2,1)S(1)}, bf16[128,128]{1,0:T(8,128)(2,1)S(1)}, u32[]{:S(2)}, u32[]{:S(2)}) collective-permute-start(bf16[128,128]{1,0:T(8,128)(2,1)S(1)} %get-tuple-element.64), channel_id=1, source_target_pairs={{0,192},{1,193},{2,194},{3,195},{4,196},{5,197},{6,198},{7,199},{8... | collective-permute-start | bytes 98312 | tf_op jit(solution)/shard_map/ppermute | solution.py:40
  128.9 4.8 %collective-permute-start.31 = (bf16[128,128]{1,0:T(8,128)(2,1)S(1)}, bf16[128,128]{1,0:T(8,128)(2,1)S(1)}, u32[]{:S(2)}, u32[]{:S(2)}) collective-permute-start(bf16[128,128]{1,0:T(8,128)(2,1)S(1)} %get-tuple-element.65), channel_id=1, source_target_pairs={{0,160},{1,161},{2,162},{3,163},{4,164},{5,165},{6,166},{7,167},{8... | collective-permute-start | bytes 98312 | tf_op jit(solution)/shard_map/ppermute | solution.py:40
  (7 other events, 176.6 us)
where the time goes:
time: 139 us
  waiting for transfers between devices  62.3 us (45%)
  starting transfers between devices  48.5 us (35%)
  Pallas kernels  26.2 us (19%)
    ppermute x32, waiting for transfers between devices, perm(): return lax.ppermute(block, AXES, pairs)  62.3 us
    ppermute x32, starting transfers between devices, perm(): return lax.ppermute(block, AXES, pairs)  48.5 us
    pallas_call x13, Pallas kernels, call(): pl.pallas_call(kernel, out_shape=shapes, in_specs=[pl.BlockSpec(memory_sp...  19.9 us
    pallas_call x1, Pallas kernels, sketch_call(): pl.pallas_call(sketch_kernel, out_shape=[pltpu.VMEM(out, BF16), pltpu.VME...  5.43 us
  transfers between devices with their start and end apart: 32, of which 17 were waited for; matrix products, arithmetic and copies ran while one was open for 0% of the time, Pallas kernels for 8%

commit v1 on v0

--- a/solution.py
+++ b/solution.py
@@ -52,11 +52,10 @@
     return (u ^ 1, c)
 
 
-def to_column(k, other):
+def to_column(k):
     def route(u, c):
-        x, core = u // 2, u % 2
         plane, y = c // NY, c % NY
-        return (2 * ((x + k) % NX) + (core ^ other), (plane + core) % NZ * NY + (y + x + 1) % NY)
+        return ((u + 2 * k) % NU, (plane + u % 2) % NZ * NY + (y + u // 2 + 1) % NY)
 
     return route
 
@@ -240,8 +239,8 @@
 
 
 def tile_kernel(sum_ref, inverse_ref, own_ref, a_ref, b_ref, c_ref, dinv_ref, *refs):
-    bundles, cross_ref, outs = refs[:5], refs[5], refs[6 : 6 + NU]
-    updated, solved = refs[6 + NU :]
+    bundles, cross_ref, outs = refs[:5], refs[5], refs[6 : 6 + NX]
+    updated, solved = refs[6 + NX :]
     x, core = place()
     raw = owner_sum(own_ref, a_ref, b_ref, c_ref)
     cross_ref[...] = dot(inverse_ref[...], raw, ((1,), (0,)), EXACT).astype(BF16)
@@ -261,19 +260,16 @@
     for k in range(NX):
         at = pl.multiple_of(((x + k) & 3) * (2 * BLK), 2 * BLK)
         product = dot(solved[pl.ds(at + wrap, 2 * BLK)], solved[pl.ds(at, (HALF + 1) * BLK)], NEAR)
-        upper = product[:BLK, : HALF * BLK].astype(BF16)
-        lower = product[BLK:, BLK:].astype(BF16)
-        on_lower = core == 1
-        outs[2 * k][...] = jnp.where(on_lower, lower, upper)
-        outs[2 * k + 1][...] = jnp.where(on_lower, upper, lower)
+        outs[k][0] = product[:BLK, : HALF * BLK].astype(BF16)
+        outs[k][1] = product[BLK:, BLK:].astype(BF16)
 
 
 def tile_call(summed, inverse, parts, dinv, rows):
     width = dinv.shape[0]
-    out = ((BLK, HALF * BLK), BF16)
+    out = ((2, BLK, HALF * BLK), BF16)
     return call(
         tile_kernel,
-        [(summed.shape, BF16)] + [out] * NU,
+        [(summed.shape, BF16)] + [out] * NX,
         [summed, inverse, *parts, dinv, *rows],
         scratch=[
             pltpu.VMEM((NX, 2 * BLK, width), BF16),
@@ -321,27 +317,39 @@
     )[0]
 
 
-def arrived_kernel(*refs):
-    refs, (here_ref, onward_ref) = refs[:NU], refs[NU:]
+def arrived_kernel(a_ref, b_ref, c_ref, d_ref, send_ref, keep_ref):
     x, core = place()
     col = lax.axis_index("col")
     y, z = col & 3, col >> 2
-    here, onward = 0.0, 0.0
-    for k in range(NX):
-        first, second = refs[2 * k][...].astype(F32), refs[2 * k + 1][...].astype(F32)
-        near = jnp.where(core == 0, first, second)
-        far = jnp.where(core == 0, second, first)
-        both = near + jnp.where(z > 0, far, 0.0)
-        stays = y > ((x - k) & 3)
-        here = here + jnp.where(stays, both, 0.0)
-        onward = onward + jnp.where(stays, 0.0, both)
-    here_ref[...] = here
-    onward_ref[...] = onward.astype(BF16)
+    valid = (core == 0) | (z > 0)
+    for other in range(2):
+        here, onward = 0.0, 0.0
+        for k, ref in enumerate((a_ref, b_ref, c_ref, d_ref)):
+            block = jnp.where(valid, ref[core ^ other].astype(F32), 0.0)
+            stays = y > ((x - k) & 3)
+            here = here + jnp.where(stays, block, 0.0)
+            onward = onward + jnp.where(stays, 0.0, block)
+        if other:
+            send_ref[0] = here.astype(BF16)
+            send_ref[1] = onward.astype(BF16)
+        else:
+            keep_ref[0] = here
+            keep_ref[1] = onward
 
 
 def arrived_sum(arrived):
     shape = arrived[0].shape
-    return call(arrived_kernel, [(shape, F32), (shape, BF16)], arrived)
+    return call(arrived_kernel, [(shape, BF16), (shape, F32)], arrived)
+
+
+def plane_kernel(keep_ref, got_ref, here_ref, onward_ref):
+    here_ref[...] = keep_ref[0] + got_ref[0].astype(F32)
+    onward_ref[...] = (keep_ref[1] + got_ref[1].astype(F32)).astype(BF16)
+
+
+def plane_sum(keep, got):
+    shape = keep.shape[1:]
+    return call(plane_kernel, [(shape, F32), (shape, BF16)], [keep, got])
 
 
 def collect_kernel(here_ref, onward_ref, total_ref, a_ref, b_ref, c_ref):
@@ -415,20 +423,17 @@
     others = shifted(others, along_x)
     tile = tile_call(own_sum, inverse, [own, *others], dinv, rows)
     cross, *blocks = tile
-    arrived = [None] * NU
-    for i in ORDER:
-        arrived[i] = perm(blocks[i], to_column(i // 2, i % 2))
+    arrived = shifted(blocks, to_column, 0)
     crosses = gathered(cross)
-    here, onward = arrived_sum(arrived)
+    send, keep = arrived_sum(arrived)
+    got = perm(send, partner)
+    here, onward = plane_sum(keep, got)
     onward = [perm(onward, along_z(1))]
     total, *mirrored = collect(here, onward)
     mirrored = shifted(mirrored, lambda d: along_upd(-d))
     panel_out = rows_call(panel, dinv, sums, crosses)
     diag_out = diag_call(diag_tiles[0], total, mirrored)
     return (panel_out[None], diag_out[None])
-
-
-ORDER = (2, 6, 3, 7, 4, 5, 0, 1)
 
 
 def solution(mesh):

time: 139 us -> 128 us (0.921)
  waiting for transfers between devices: 62.3 us -> 52 us
    ppermute x32 -> x29, waiting for transfers between devices: 62.3 us -> 52 us  [perm(): return lax.ppermute(block, AXES, pairs)]
    ppermute x32 -> x29, starting transfers between devices: 48.5 us -> 47.6 us  [perm(): return lax.ppermute(block, AXES, pairs)]
    pallas_call x13 -> x14, Pallas kernels: 19.9 us -> 20 us  [call(): pl.pallas_call(kernel, out_shape=shapes, in_specs=[pl.BlockSpec(memory_sp...]
  transfers between devices with their start and end apart: 32 -> 29, of which waited for: 17 -> 14; matrix products, arithmetic and copies ran while one was open for 0% -> 0% of each run, Pallas kernels for 8% -> 11%
where the time goes in v1:
time: 128 us
  waiting for transfers between devices  52 us (41%)
  starting transfers between devices  47.6 us (37%)
  Pallas kernels  26.3 us (21%)
    ppermute x29, waiting for transfers between devices, perm(): return lax.ppermute(block, AXES, pairs)  52 us
    ppermute x29, starting transfers between devices, perm(): return lax.ppermute(block, AXES, pairs)  47.6 us
    pallas_call x14, Pallas kernels, call(): pl.pallas_call(kernel, out_shape=shapes, in_specs=[pl.BlockSpec(memory_sp...  20 us
    pallas_call x1, Pallas kernels, sketch_call(): pl.pallas_call(sketch_kernel, out_shape=[pltpu.VMEM(out, BF16), pltpu.VME...  5.43 us
  transfers between devices with their start and end apart: 29, of which 14 were waited for; matrix products, arithmetic and copies ran while one was open for 0% of the time, Pallas kernels for 11%

profile of v1, /device:TPU:1, one launch (start us, length us, event | category | flops | bytes accessed | tf_op | source)
XLA Modules:
  0.0 127.5 jit_solution(4340558984941541389)
XLA Ops:
  1.4 5.4 %sketch_product.1 = (bf16[4,64,1024]{2,1,0:T(8,128)(2,1)S(1)}, f32[4,64,1024]{2,1,0:T(8,128)S(1)}) custom-call(s32[8]{0:T(128)S(1)} %bitcast.18, bf16[8,96,1024]{2,1,0:T(8,128)(2,1)} %bitcast.13, bf16[8,96,1024]{2,1,0:T(8,128)(2,1)} %bitcast.15, bf16[64,1024]{1,0:T(8,128)(2,1)} %bitcast.22), custom_call_target="tpu_custom_call" | custom-call | tf_op jit(solution)/shard_map/sketch_product/pallas_call | solution.py:120
  6.9 3.3 %collective-permute-start = (bf16[4,64,1024]{2,1,0:T(8,128)(2,1)S(1)}, bf16[4,64,1024]{2,1,0:T(8,128)(2,1)S(1)}, u32[]{:S(2)}, u32[]{:S(2)}) collective-permute-start(bf16[4,64,1024]{2,1,0:T(8,128)(2,1)S(1)} %get-tuple-element.33), channel_id=1, source_target_pairs={{0,32},{1,33},{2,34},{3,35},{4,36},{5,37},{6,38},{7,39},{8,40},{9,... | collective-permute-start | bytes 1572872 | tf_op jit(solution)/shard_map/ppermute | solution.py:40
  10.5 1.2 collective-permute-done.got_ref
  11.9 1.9 %collective-permute-start.2 = (bf16[64,1024]{1,0:T(8,128)(2,1)S(1)}, bf16[64,1024]{1,0:T(8,128)(2,1)S(1)}, u32[]{:S(2)}, u32[]{:S(2)}) collective-permute-start(bf16[64,1024]{1,0:T(8,128)(2,1)S(1)} %get-tuple-element.36), channel_id=1, source_target_pairs={{0,128},{1,129},{2,130},{3,131},{4,132},{5,133},{6,134},{7,135},{8... | collective-permute-start | bytes 393224 | tf_op jit(solution)/shard_map/ppermute | solution.py:40
  13.9 1.2 collective-permute-start.3
  15.0 3.5 %collective-permute-done.1.a_ref = bf16[64,1024]{1,0:T(8,128)(2,1)S(1)} collective-permute-done((bf16[64,1024]{1,0:T(8,128)(2,1)S(1)}, bf16[64,1024]{1,0:T(8,128)(2,1)S(1)}, u32[]{:S(2)}, u32[]{:S(2)}) %collective-permute-start.1) | collective-permute-done | bytes 131104 | tf_op jit(solution)/shard_map/ppermute | solution.py:40
  18.5 1.4 %collective-permute-done.2.b_ref = bf16[64,1024]{1,0:T(8,128)(2,1)S(1)} collective-permute-done((bf16[64,1024]{1,0:T(8,128)(2,1)S(1)}, bf16[64,1024]{1,0:T(8,128)(2,1)S(1)}, u32[]{:S(2)}, u32[]{:S(2)}) %collective-permute-start.2) | collective-permute-done | bytes 131104 | tf_op jit(solution)/shard_map/ppermute | solution.py:40
  21.0 3.5 %collective-permute-start.6 = (bf16[64,1024]{1,0:T(8,128)(2,1)S(1)}, bf16[64,1024]{1,0:T(8,128)(2,1)S(1)}, u32[]{:S(2)}, u32[]{:S(2)}) collective-permute-start(bf16[64,1024]{1,0:T(8,128)(2,1)S(1)} %shard_map.87.a_ref.summed_ref.refs_0_.sum_ref), channel_id=1, source_target_pairs={{0,192},{1,193},{2,194},{3,195},{4,196},{5,197},{6,198},{7,199},{8... | collective-permute-start | bytes 393224 | tf_op jit(solution)/shard_map/ppermute | solution.py:40
  25.1 4.6 %collective-permute-done.6.d_ref.refs_3_ = bf16[64,1024]{1,0:T(8,128)(2,1)S(1)} collective-permute-done((bf16[64,1024]{1,0:T(8,128)(2,1)S(1)}, bf16[64,1024]{1,0:T(8,128)(2,1)S(1)}, u32[]{:S(2)}, u32[]{:S(2)}) %collective-permute-start.6) | collective-permute-done | bytes 131104 | tf_op jit(solution)/shard_map/ppermute | solution.py:40
  30.3 3.3 %collective-permute-done.4.b_ref.refs_1_ = bf16[64,1024]{1,0:T(8,128)(2,1)S(1)} collective-permute-done((bf16[64,1024]{1,0:T(8,128)(2,1)S(1)}, bf16[64,1024]{1,0:T(8,128)(2,1)S(1)}, u32[]{:S(2)}, u32[]{:S(2)}) %collective-permute-start.4) | collective-permute-done | bytes 131104 | tf_op jit(solution)/shard_map/ppermute | solution.py:40
  34.5 1.5 %collective-permute-done.7.refs_4_ = bf16[4,64,1024]{2,1,0:T(8,128)(2,1)S(1)} collective-permute-done((bf16[4,64,1024]{2,1,0:T(8,128)(2,1)S(1)}, bf16[4,64,1024]{2,1,0:T(8,128)(2,1)S(1)}, u32[]{:S(2)}, u32[]{:S(2)}) %collective-permute-start.7) | collective-permute-done | bytes 524320 | tf_op jit(solution)/shard_map/ppermute | solution.py:40
  36.1 3.1 %shard_map.90 = (bf16[4,64,1024]{2,1,0:T(8,128)(2,1)S(1)}, f32[4,64,1024]{2,1,0:T(8,128)S(1)}) custom-call(s32[8]{0:T(128)S(1)} %bitcast.19, bf16[8,96,1024]{2,1,0:T(8,128)(2,1)S(1)} %bitcast.16, bf16[8,96,1024]{2,1,0:T(8,128)(2,1)S(1)} %bitcast.14, bf16[64,1024]{1,0:T(8,128)(2,1)S(1)} %shard_map.87.a_ref.summed_ref.refs_0_.sum_ref, ...), custom_call_target="tpu_custom_call" | custom-call | tf_op jit(solution)/shard_map/pallas_call | solution.py:74
  39.8 1.8 %collective-permute-start.14 = (bf16[2,128,1024]{2,1,0:T(8,128)(2,1)S(1)}, bf16[2,128,1024]{2,1,0:T(8,128)(2,1)S(1)}, u32[]{:S(2)}, u32[]{:S(2)}) collective-permute-start(bf16[2,128,1024]{2,1,0:T(8,128)(2,1)S(1)} %get-tuple-element.47), channel_id=1, source_target_pairs={{0,128},{1,129},{2,130},{3,131},{4,132},{5,133},{6,134},{7,135},{8... | collective-permute-start | bytes 1572872 | tf_op jit(solution)/shard_map/ppermute | solution.py:40
  43.4 1.9 %collective-permute-start.10 = (bf16[64,1024]{1,0:T(8,128)(2,1)S(1)}, bf16[64,1024]{1,0:T(8,128)(2,1)S(1)}, u32[]{:S(2)}, u32[]{:S(2)}) collective-permute-start(bf16[64,1024]{1,0:T(8,128)(2,1)S(1)} %get-tuple-element.42), channel_id=1, source_target_pairs={{0,128},{1,129},{2,130},{3,131},{4,132},{5,133},{6,134},{7,135},{8... | collective-permute-start | bytes 393224 | tf_op jit(solution)/shard_map/ppermute | solution.py:40
  45.3 19.9 %collective-permute-done.13.refs_2_ = bf16[2,128,1024]{2,1,0:T(8,128)(2,1)S(1)} collective-permute-done((bf16[2,128,1024]{2,1,0:T(8,128)(2,1)S(1)}, bf16[2,128,1024]{2,1,0:T(8,128)(2,1)S(1)}, u32[]{:S(2)}, u32[]{:S(2)}) %collective-permute-start.13) | collective-permute-done | bytes 524320 | tf_op jit(solution)/shard_map/ppermute | solution.py:40
  65.2 6.1 %shard_map.89.inverse_ref = f32[64,64]{1,0:T(8,128)S(1)} custom-call(bf16[64,1024]{1,0:T(8,128)(2,1)S(1)} %shard_map.87.a_ref.summed_ref.refs_0_.sum_ref), custom_call_target="tpu_custom_call" | custom-call | tf_op jit(solution)/shard_map/pallas_call | solution.py:74
  71.6 5.6 %shard_map.94 = (bf16[64,1024]{1,0:T(8,128)(2,1)S(1)}, bf16[2,128,640]{2,1,0:T(8,128)(2,1)S(1)}, bf16[2,128,640]{2,1,0:T(8,128)(2,1)S(1)}, bf16[2,128,640]{2,1,0:T(8,128)(2,1)S(1)}, bf16[2,128,640]{2,1,0:T(8,128)(2,1)S(1)}) custom-call(bf16[64,1024]{1,0:T(8,128)(2,1)S(1)} %shard_map.87.a_ref.summed_ref.refs_0_.sum_ref, f32[64,64]{1,0:T(8,128)S(1)} %shard_map.89.inverse_ref, ...), custom_call_target="tpu_custom_call" | custom-call | tf_op jit(solution)/shard_map/pallas_call | solution.py:74
  77.2 2.7 %collective-permute-start.20 = (bf16[2,128,640]{2,1,0:T(8,128)(2,1)S(1)}, bf16[2,128,640]{2,1,0:T(8,128)(2,1)S(1)}, u32[]{:S(2)}, u32[]{:S(2)}) collective-permute-start(bf16[2,128,640]{2,1,0:T(8,128)(2,1)S(1)} %get-tuple-element.50), channel_id=1, source_target_pairs={{0,1},{1,2},{2,3},{3,0},{4,5},{5,6},{6,7},{7,4},{8,9},{9,10},{10,1... | collective-permute-start | bytes 983048 | tf_op jit(solution)/shard_map/ppermute | solution.py:40
  79.9 4.6 %collective-permute-start.21 = (bf16[2,128,640]{2,1,0:T(8,128)(2,1)S(1)}, bf16[2,128,640]{2,1,0:T(8,128)(2,1)S(1)}, u32[]{:S(2)}, u32[]{:S(2)}) collective-permute-start(bf16[2,128,640]{2,1,0:T(8,128)(2,1)S(1)} %get-tuple-element.51), channel_id=1, source_target_pairs={{0,65},{1,66},{2,67},{3,64},{4,69},{5,70},{6,71},{7,68},{8,73},{9,... | collective-permute-start | bytes 983048 | tf_op jit(solution)/shard_map/ppermute | solution.py:40
  84.5 1.9 %collective-permute-start.22 = (bf16[2,128,640]{2,1,0:T(8,128)(2,1)S(1)}, bf16[2,128,640]{2,1,0:T(8,128)(2,1)S(1)}, u32[]{:S(2)}, u32[]{:S(2)}) collective-permute-start(bf16[2,128,640]{2,1,0:T(8,128)(2,1)S(1)} %get-tuple-element.52), channel_id=1, source_target_pairs={{0,129},{1,130},{2,131},{3,128},{4,133},{5,134},{6,135},{7,132},{8... | collective-permute-start | bytes 983048 | tf_op jit(solution)/shard_map/ppermute | solution.py:40
  86.4 3.5 %collective-permute-start.23 = (bf16[2,128,640]{2,1,0:T(8,128)(2,1)S(1)}, bf16[2,128,640]{2,1,0:T(8,128)(2,1)S(1)}, u32[]{:S(2)}, u32[]{:S(2)}) collective-permute-start(bf16[2,128,640]{2,1,0:T(8,128)(2,1)S(1)} %get-tuple-element.53), channel_id=1, source_target_pairs={{0,193},{1,194},{2,195},{3,192},{4,197},{5,198},{6,199},{7,196},{8... | collective-permute-start | bytes 983048 | tf_op jit(solution)/shard_map/ppermute | solution.py:40
  89.9 3.8 %collective-permute-start.18 = (bf16[64,1024]{1,0:T(8,128)(2,1)S(1)}, bf16[64,1024]{1,0:T(8,128)(2,1)S(1)}, u32[]{:S(2)}, u32[]{:S(2)}) collective-permute-start(bf16[64,1024]{1,0:T(8,128)(2,1)S(1)} %get-tuple-element.49.a_ref.refs_5_), channel_id=1, source_target_pairs={{0,192},{1,193},{2,194},{3,195},{4,196},{5,197},{6,198},{7,199},{8... | collective-permute-start | bytes 393224 | tf_op jit(solution)/shard_map/ppermute | solution.py:40
  93.7 1.2 collective-permute-start.17
  94.9 2.1 %collective-permute-start.16 = (bf16[64,1024]{1,0:T(8,128)(2,1)S(1)}, bf16[64,1024]{1,0:T(8,128)(2,1)S(1)}, u32[]{:S(2)}, u32[]{:S(2)}) collective-permute-start(bf16[64,1024]{1,0:T(8,128)(2,1)S(1)} %get-tuple-element.49.a_ref.refs_5_), channel_id=1, source_target_pairs={{0,64},{1,65},{2,66},{3,67},{4,68},{5,69},{6,70},{7,71},{8,72},{9,... | collective-permute-start | bytes 393224 | tf_op jit(solution)/shard_map/ppermute | solution.py:40
  97.0 1.2 collective-permute-done.22.c_ref
  98.2 4.5 %collective-permute-done.23.d_ref = bf16[2,128,640]{2,1,0:T(8,128)(2,1)S(1)} collective-permute-done((bf16[2,128,640]{2,1,0:T(8,128)(2,1)S(1)}, bf16[2,128,640]{2,1,0:T(8,128)(2,1)S(1)}, u32[]{:S(2)}, u32[]{:S(2)}) %collective-permute-start.23) | collective-permute-done | bytes 327712 | tf_op jit(solution)/shard_map/ppermute | solution.py:40
  103.2 3.3 %collective-permute-start.24 = (bf16[2,128,640]{2,1,0:T(8,128)(2,1)S(1)}, bf16[2,128,640]{2,1,0:T(8,128)(2,1)S(1)}, u32[]{:S(2)}, u32[]{:S(2)}) collective-permute-start(bf16[2,128,640]{2,1,0:T(8,128)(2,1)S(1)} %get-tuple-element.55), channel_id=1, source_target_pairs={{0,32},{1,33},{2,34},{3,35},{4,36},{5,37},{6,38},{7,39},{8,40},{9,... | collective-permute-start | bytes 983048 | tf_op jit(solution)/shard_map/ppermute | solution.py:40
  106.5 1.2 collective-permute-start.19
  107.8 2.1 %collective-permute-start.25 = (bf16[128,640]{1,0:T(8,128)(2,1)S(1)}, bf16[128,640]{1,0:T(8,128)(2,1)S(1)}, u32[]{:S(2)}, u32[]{:S(2)}) collective-permute-start(bf16[128,640]{1,0:T(8,128)(2,1)S(1)} %get-tuple-element.57), channel_id=1, source_target_pairs={{0,4},{1,5},{2,6},{3,7},{4,8},{5,9},{6,10},{7,11},{8,12},{9,13},{1... | collective-permute-start | bytes 491528 | tf_op jit(solution)/shard_map/ppermute | solution.py:40
  109.9 8.2 %collective-permute-done.25.onward_ref = bf16[128,640]{1,0:T(8,128)(2,1)S(1)} collective-permute-done((bf16[128,640]{1,0:T(8,128)(2,1)S(1)}, bf16[128,640]{1,0:T(8,128)(2,1)S(1)}, u32[]{:S(2)}, u32[]{:S(2)}) %collective-permute-start.25) | collective-permute-done | bytes 163872 | tf_op jit(solution)/shard_map/ppermute | solution.py:40
  118.8 3.0 %collective-permute-start.27 = (bf16[128,128]{1,0:T(8,128)(2,1)S(1)}, bf16[128,128]{1,0:T(8,128)(2,1)S(1)}, u32[]{:S(2)}, u32[]{:S(2)}) collective-permute-start(bf16[128,128]{1,0:T(8,128)(2,1)S(1)} %get-tuple-element.60), channel_id=1, source_target_pairs={{0,192},{1,193},{2,194},{3,195},{4,196},{5,197},{6,198},{7,199},{8... | collective-permute-start | bytes 98312 | tf_op jit(solution)/shard_map/ppermute | solution.py:40
  121.9 4.0 %shard_map.96 = bf16[8,128,1024]{2,1,0:T(8,128)(2,1)} custom-call(bf16[8,128,1024]{2,1,0:T(8,128)(2,1)S(1)} %bitcast.12, bf16[1024,1024]{1,0:T(8,128)(2,1)S(1)} %bitcast.10, bf16[64,1024]{1,0:T(8,128)(2,1)S(1)} %shard_map.87.a_ref.summed_ref.refs_0_.sum_ref, bf16[64,1024]{1,0:T(8,128)(2,1)S(1)} %collective-permute-done.4.b_ref.refs_1_, ...), custom_call_target="tpu_custom_call" | custom-call | tf_op jit(solution)/shard_map/pallas_call | solution.py:74
  (56 shorter events, 10.2 us)
Async XLA Ops:
  6.9 4.8 %collective-permute-start = (bf16[4,64,1024]{2,1,0:T(8,128)(2,1)S(1)}, bf16[4,64,1024]{2,1,0:T(8,128)(2,1)S(1)}, u32[]{:S(2)}, u32[]{:S(2)}) collective-permute-start(bf16[4,64,1024]{2,1,0:T(8,128)(2,1)S(1)} %get-tuple-element.33), channel_id=1, source_target_pairs={{0,32},{1,33},{2,34},{3,35},{4,36},{5,37},{6,38},{7,39},{8,40},{9,... | collective-permute-start | bytes 1572872 | tf_op jit(solution)/shard_map/ppermute | solution.py:40
  10.3 25.7 %copy-start.2 = (bf16[1,8,1,96,1024]{4,3,2,1,0:T(8,128)(2,1)S(1)}, bf16[1,8,1,96,1024]{4,3,2,1,0:T(8,128)(2,1)}, u32[]{:S(2)}) copy-start(bf16[1,8,1,96,1024]{4,3,2,1,0:T(8,128)(2,1)} %param.11) | copy-start | bytes 4718596
  10.3 25.7 %copy-start.3 = (bf16[1,8,1,96,1024]{4,3,2,1,0:T(8,128)(2,1)S(1)}, bf16[1,8,1,96,1024]{4,3,2,1,0:T(8,128)(2,1)}, u32[]{:S(2)}) copy-start(bf16[1,8,1,96,1024]{4,3,2,1,0:T(8,128)(2,1)} %param.10) | copy-start | bytes 4718596
  10.4 29.3 %collective-permute-start.12 = (bf16[4,128,1024]{2,1,0:T(8,128)(2,1)S(1)}, bf16[4,128,1024]{2,1,0:T(8,128)(2,1)S(1)}, u32[]{:S(2)}, u32[]{:S(2)}) collective-permute-start(bf16[4,128,1024]{2,1,0:T(8,128)(2,1)S(1)} %get-tuple-element.45), channel_id=1, source_target_pairs={{0,32},{1,33},{2,34},{3,35},{4,36},{5,37},{6,38},{7,39},{8,40},{9,... | collective-permute-start | bytes 3145736 | tf_op jit(solution)/shard_map/ppermute | solution.py:40
  11.8 6.7 %collective-permute-start.1 = (bf16[64,1024]{1,0:T(8,128)(2,1)S(1)}, bf16[64,1024]{1,0:T(8,128)(2,1)S(1)}, u32[]{:S(2)}, u32[]{:S(2)}) collective-permute-start(bf16[64,1024]{1,0:T(8,128)(2,1)S(1)} %get-tuple-element.35), channel_id=1, source_target_pairs={{0,64},{1,65},{2,66},{3,67},{4,68},{5,69},{6,70},{7,71},{8,72},{9,... | collective-permute-start | bytes 393224 | tf_op jit(solution)/shard_map/ppermute | solution.py:40
  11.9 8.0 %collective-permute-start.2 = (bf16[64,1024]{1,0:T(8,128)(2,1)S(1)}, bf16[64,1024]{1,0:T(8,128)(2,1)S(1)}, u32[]{:S(2)}, u32[]{:S(2)}) collective-permute-start(bf16[64,1024]{1,0:T(8,128)(2,1)S(1)} %get-tuple-element.36), channel_id=1, source_target_pairs={{0,128},{1,129},{2,130},{3,131},{4,132},{5,133},{6,134},{7,135},{8... | collective-permute-start | bytes 393224 | tf_op jit(solution)/shard_map/ppermute | solution.py:40
  13.9 7.0 %collective-permute-start.3 = (bf16[64,1024]{1,0:T(8,128)(2,1)S(1)}, bf16[64,1024]{1,0:T(8,128)(2,1)S(1)}, u32[]{:S(2)}, u32[]{:S(2)}) collective-permute-start(bf16[64,1024]{1,0:T(8,128)(2,1)S(1)} %get-tuple-element.37), channel_id=1, source_target_pairs={{0,192},{1,193},{2,194},{3,195},{4,196},{5,197},{6,198},{7,199},{8... | collective-permute-start | bytes 393224 | tf_op jit(solution)/shard_map/ppermute | solution.py:40
  21.0 8.8 %collective-permute-start.6 = (bf16[64,1024]{1,0:T(8,128)(2,1)S(1)}, bf16[64,1024]{1,0:T(8,128)(2,1)S(1)}, u32[]{:S(2)}, u32[]{:S(2)}) collective-permute-start(bf16[64,1024]{1,0:T(8,128)(2,1)S(1)} %shard_map.87.a_ref.summed_ref.refs_0_.sum_ref), channel_id=1, source_target_pairs={{0,192},{1,193},{2,194},{3,195},{4,196},{5,197},{6,198},{7,199},{8... | collective-permute-start | bytes 393224 | tf_op jit(solution)/shard_map/ppermute | solution.py:40
  24.5 5.9 %collective-permute-start.5 = (bf16[64,1024]{1,0:T(8,128)(2,1)S(1)}, bf16[64,1024]{1,0:T(8,128)(2,1)S(1)}, u32[]{:S(2)}, u32[]{:S(2)}) collective-permute-start(bf16[64,1024]{1,0:T(8,128)(2,1)S(1)} %shard_map.87.a_ref.summed_ref.refs_0_.sum_ref), channel_id=1, source_target_pairs={{0,128},{1,129},{2,130},{3,131},{4,132},{5,133},{6,134},{7,135},{8... | collective-permute-start | bytes 393224 | tf_op jit(solution)/shard_map/ppermute | solution.py:40
  24.5 9.1 %collective-permute-start.4 = (bf16[64,1024]{1,0:T(8,128)(2,1)S(1)}, bf16[64,1024]{1,0:T(8,128)(2,1)S(1)}, u32[]{:S(2)}, u32[]{:S(2)}) collective-permute-start(bf16[64,1024]{1,0:T(8,128)(2,1)S(1)} %shard_map.87.a_ref.summed_ref.refs_0_.sum_ref), channel_id=1, source_target_pairs={{0,64},{1,65},{2,66},{3,67},{4,68},{5,69},{6,70},{7,71},{8,72},{9,... | collective-permute-start | bytes 393224 | tf_op jit(solution)/shard_map/ppermute | solution.py:40
  33.6 2.4 %collective-permute-start.7 = (bf16[4,64,1024]{2,1,0:T(8,128)(2,1)S(1)}, bf16[4,64,1024]{2,1,0:T(8,128)(2,1)S(1)}, u32[]{:S(2)}, u32[]{:S(2)}) collective-permute-start(bf16[4,64,1024]{2,1,0:T(8,128)(2,1)S(1)} %shard_map.88), channel_id=1, source_target_pairs={{0,32},{1,33},{2,34},{3,35},{4,36},{5,37},{6,38},{7,39},{8,40},{9,... | collective-permute-start | bytes 1572872 | tf_op jit(solution)/shard_map/ppermute | solution.py:40
  39.1 32.5 %copy-start = (bf16[1,1024,1024]{2,1,0:T(8,128)(2,1)S(1)}, bf16[1,1024,1024]{2,1,0:T(8,128)(2,1)}, u32[]{:S(2)}) copy-start(bf16[1,1024,1024]{2,1,0:T(8,128)(2,1)} %param.9) | copy-start | bytes 6291460
  39.2 3.3 %collective-permute-start.8 = (bf16[4,64,1024]{2,1,0:T(8,128)(2,1)S(1)}, bf16[4,64,1024]{2,1,0:T(8,128)(2,1)S(1)}, u32[]{:S(2)}, u32[]{:S(2)}) collective-permute-start(bf16[4,64,1024]{2,1,0:T(8,128)(2,1)S(1)} %get-tuple-element.39), channel_id=1, source_target_pairs={{0,32},{1,33},{2,34},{3,35},{4,36},{5,37},{6,38},{7,39},{8,40},{9,... | collective-permute-start | bytes 1572872 | tf_op jit(solution)/shard_map/ppermute | solution.py:40
  39.7 25.5 %collective-permute-start.13 = (bf16[2,128,1024]{2,1,0:T(8,128)(2,1)S(1)}, bf16[2,128,1024]{2,1,0:T(8,128)(2,1)S(1)}, u32[]{:S(2)}, u32[]{:S(2)}) collective-permute-start(bf16[2,128,1024]{2,1,0:T(8,128)(2,1)S(1)} %get-tuple-element.46), channel_id=1, source_target_pairs={{0,64},{1,65},{2,66},{3,67},{4,68},{5,69},{6,70},{7,71},{8,72},{9,... | collective-permute-start | bytes 1572872 | tf_op jit(solution)/shard_map/ppermute | solution.py:40
  39.8 31.5 %collective-permute-start.14 = (bf16[2,128,1024]{2,1,0:T(8,128)(2,1)S(1)}, bf16[2,128,1024]{2,1,0:T(8,128)(2,1)S(1)}, u32[]{:S(2)}, u32[]{:S(2)}) collective-permute-start(bf16[2,128,1024]{2,1,0:T(8,128)(2,1)S(1)} %get-tuple-element.47), channel_id=1, source_target_pairs={{0,128},{1,129},{2,130},{3,131},{4,132},{5,133},{6,134},{7,135},{8... | collective-permute-start | bytes 1572872 | tf_op jit(solution)/shard_map/ppermute | solution.py:40
  41.6 29.7 %collective-permute-start.15 = (bf16[2,128,1024]{2,1,0:T(8,128)(2,1)S(1)}, bf16[2,128,1024]{2,1,0:T(8,128)(2,1)S(1)}, u32[]{:S(2)}, u32[]{:S(2)}) collective-permute-start(bf16[2,128,1024]{2,1,0:T(8,128)(2,1)S(1)} %get-tuple-element.48), channel_id=1, source_target_pairs={{0,192},{1,193},{2,194},{3,195},{4,196},{5,197},{6,198},{7,199},{8... | collective-permute-start | bytes 1572872 | tf_op jit(solution)/shard_map/ppermute | solution.py:40
  42.6 28.8 %collective-permute-start.9 = (bf16[64,1024]{1,0:T(8,128)(2,1)S(1)}, bf16[64,1024]{1,0:T(8,128)(2,1)S(1)}, u32[]{:S(2)}, u32[]{:S(2)}) collective-permute-start(bf16[64,1024]{1,0:T(8,128)(2,1)S(1)} %get-tuple-element.41), channel_id=1, source_target_pairs={{0,64},{1,65},{2,66},{3,67},{4,68},{5,69},{6,70},{7,71},{8,72},{9,... | collective-permute-start | bytes 393224 | tf_op jit(solution)/shard_map/ppermute | solution.py:40
  43.4 27.9 %collective-permute-start.10 = (bf16[64,1024]{1,0:T(8,128)(2,1)S(1)}, bf16[64,1024]{1,0:T(8,128)(2,1)S(1)}, u32[]{:S(2)}, u32[]{:S(2)}) collective-permute-start(bf16[64,1024]{1,0:T(8,128)(2,1)S(1)} %get-tuple-element.42), channel_id=1, source_target_pairs={{0,128},{1,129},{2,130},{3,131},{4,132},{5,133},{6,134},{7,135},{8... | collective-permute-start | bytes 393224 | tf_op jit(solution)/shard_map/ppermute | solution.py:40
  65.2 6.4 %collective-permute-start.11 = (bf16[64,1024]{1,0:T(8,128)(2,1)S(1)}, bf16[64,1024]{1,0:T(8,128)(2,1)S(1)}, u32[]{:S(2)}, u32[]{:S(2)}) collective-permute-start(bf16[64,1024]{1,0:T(8,128)(2,1)S(1)} %get-tuple-element.43), channel_id=1, source_target_pairs={{0,192},{1,193},{2,194},{3,195},{4,196},{5,197},{6,198},{7,199},{8... | collective-permute-start | bytes 393224 | tf_op jit(solution)/shard_map/ppermute | solution.py:40
  77.2 16.5 %collective-permute-start.20 = (bf16[2,128,640]{2,1,0:T(8,128)(2,1)S(1)}, bf16[2,128,640]{2,1,0:T(8,128)(2,1)S(1)}, u32[]{:S(2)}, u32[]{:S(2)}) collective-permute-start(bf16[2,128,640]{2,1,0:T(8,128)(2,1)S(1)} %get-tuple-element.50), channel_id=1, source_target_pairs={{0,1},{1,2},{2,3},{3,0},{4,5},{5,6},{6,7},{7,4},{8,9},{9,10},{10,1... | collective-permute-start | bytes 983048 | tf_op jit(solution)/shard_map/ppermute | solution.py:40
  79.9 15.0 %collective-permute-start.21 = (bf16[2,128,640]{2,1,0:T(8,128)(2,1)S(1)}, bf16[2,128,640]{2,1,0:T(8,128)(2,1)S(1)}, u32[]{:S(2)}, u32[]{:S(2)}) collective-permute-start(bf16[2,128,640]{2,1,0:T(8,128)(2,1)S(1)} %get-tuple-element.51), channel_id=1, source_target_pairs={{0,65},{1,66},{2,67},{3,64},{4,69},{5,70},{6,71},{7,68},{8,73},{9,... | collective-permute-start | bytes 983048 | tf_op jit(solution)/shard_map/ppermute | solution.py:40
  84.5 13.7 %collective-permute-start.22 = (bf16[2,128,640]{2,1,0:T(8,128)(2,1)S(1)}, bf16[2,128,640]{2,1,0:T(8,128)(2,1)S(1)}, u32[]{:S(2)}, u32[]{:S(2)}) collective-permute-start(bf16[2,128,640]{2,1,0:T(8,128)(2,1)S(1)} %get-tuple-element.52), channel_id=1, source_target_pairs={{0,129},{1,130},{2,131},{3,128},{4,133},{5,134},{6,135},{7,132},{8... | collective-permute-start | bytes 983048 | tf_op jit(solution)/shard_map/ppermute | solution.py:40
  86.4 16.3 %collective-permute-start.23 = (bf16[2,128,640]{2,1,0:T(8,128)(2,1)S(1)}, bf16[2,128,640]{2,1,0:T(8,128)(2,1)S(1)}, u32[]{:S(2)}, u32[]{:S(2)}) collective-permute-start(bf16[2,128,640]{2,1,0:T(8,128)(2,1)S(1)} %get-tuple-element.53), channel_id=1, source_target_pairs={{0,193},{1,194},{2,195},{3,192},{4,197},{5,198},{6,199},{7,196},{8... | collective-permute-start | bytes 983048 | tf_op jit(solution)/shard_map/ppermute | solution.py:40
  89.9 16.6 %collective-permute-start.18 = (bf16[64,1024]{1,0:T(8,128)(2,1)S(1)}, bf16[64,1024]{1,0:T(8,128)(2,1)S(1)}, u32[]{:S(2)}, u32[]{:S(2)}) collective-permute-start(bf16[64,1024]{1,0:T(8,128)(2,1)S(1)} %get-tuple-element.49.a_ref.refs_5_), channel_id=1, source_target_pairs={{0,192},{1,193},{2,194},{3,195},{4,196},{5,197},{6,198},{7,199},{8... | collective-permute-start | bytes 393224 | tf_op jit(solution)/shard_map/ppermute | solution.py:40
  93.7 12.8 %collective-permute-start.17 = (bf16[64,1024]{1,0:T(8,128)(2,1)S(1)}, bf16[64,1024]{1,0:T(8,128)(2,1)S(1)}, u32[]{:S(2)}, u32[]{:S(2)}) collective-permute-start(bf16[64,1024]{1,0:T(8,128)(2,1)S(1)} %get-tuple-element.49.a_ref.refs_5_), channel_id=1, source_target_pairs={{0,128},{1,129},{2,130},{3,131},{4,132},{5,133},{6,134},{7,135},{8... | collective-permute-start | bytes 393224 | tf_op jit(solution)/shard_map/ppermute | solution.py:40
  94.9 11.6 %collective-permute-start.16 = (bf16[64,1024]{1,0:T(8,128)(2,1)S(1)}, bf16[64,1024]{1,0:T(8,128)(2,1)S(1)}, u32[]{:S(2)}, u32[]{:S(2)}) collective-permute-start(bf16[64,1024]{1,0:T(8,128)(2,1)S(1)} %get-tuple-element.49.a_ref.refs_5_), channel_id=1, source_target_pairs={{0,64},{1,65},{2,66},{3,67},{4,68},{5,69},{6,70},{7,71},{8,72},{9,... | collective-permute-start | bytes 393224 | tf_op jit(solution)/shard_map/ppermute | solution.py:40
  103.2 4.5 %collective-permute-start.24 = (bf16[2,128,640]{2,1,0:T(8,128)(2,1)S(1)}, bf16[2,128,640]{2,1,0:T(8,128)(2,1)S(1)}, u32[]{:S(2)}, u32[]{:S(2)}) collective-permute-start(bf16[2,128,640]{2,1,0:T(8,128)(2,1)S(1)} %get-tuple-element.55), channel_id=1, source_target_pairs={{0,32},{1,33},{2,34},{3,35},{4,36},{5,37},{6,38},{7,39},{8,40},{9,... | collective-permute-start | bytes 983048 | tf_op jit(solution)/shard_map/ppermute | solution.py:40
  106.5 15.4 %collective-permute-start.19 = (bf16[4,64,1024]{2,1,0:T(8,128)(2,1)S(1)}, bf16[4,64,1024]{2,1,0:T(8,128)(2,1)S(1)}, u32[]{:S(2)}, u32[]{:S(2)}) collective-permute-start(bf16[4,64,1024]{2,1,0:T(8,128)(2,1)S(1)} %shard_map.95), channel_id=1, source_target_pairs={{0,32},{1,33},{2,34},{3,35},{4,36},{5,37},{6,38},{7,39},{8,40},{9,... | collective-permute-start | bytes 1572872 | tf_op jit(solution)/shard_map/ppermute | solution.py:40
  107.8 10.3 %collective-permute-start.25 = (bf16[128,640]{1,0:T(8,128)(2,1)S(1)}, bf16[128,640]{1,0:T(8,128)(2,1)S(1)}, u32[]{:S(2)}, u32[]{:S(2)}) collective-permute-start(bf16[128,640]{1,0:T(8,128)(2,1)S(1)} %get-tuple-element.57), channel_id=1, source_target_pairs={{0,4},{1,5},{2,6},{3,7},{4,8},{5,9},{6,10},{7,11},{8,12},{9,13},{1... | collective-permute-start | bytes 491528 | tf_op jit(solution)/shard_map/ppermute | solution.py:40
  118.2 7.8 %collective-permute-start.26 = (bf16[128,128]{1,0:T(8,128)(2,1)S(1)}, bf16[128,128]{1,0:T(8,128)(2,1)S(1)}, u32[]{:S(2)}, u32[]{:S(2)}) collective-permute-start(bf16[128,128]{1,0:T(8,128)(2,1)S(1)} %get-tuple-element.59), channel_id=1, source_target_pairs={{0,224},{1,225},{2,226},{3,227},{4,228},{5,229},{6,230},{7,231},{8... | collective-permute-start | bytes 98312 | tf_op jit(solution)/shard_map/ppermute | solution.py:40
  118.8 7.2 %collective-permute-start.27 = (bf16[128,128]{1,0:T(8,128)(2,1)S(1)}, bf16[128,128]{1,0:T(8,128)(2,1)S(1)}, u32[]{:S(2)}, u32[]{:S(2)}) collective-permute-start(bf16[128,128]{1,0:T(8,128)(2,1)S(1)} %get-tuple-element.60), channel_id=1, source_target_pairs={{0,192},{1,193},{2,194},{3,195},{4,196},{5,197},{6,198},{7,199},{8... | collective-permute-start | bytes 98312 | tf_op jit(solution)/shard_map/ppermute | solution.py:40
  121.8 4.8 %collective-permute-start.28 = (bf16[128,128]{1,0:T(8,128)(2,1)S(1)}, bf16[128,128]{1,0:T(8,128)(2,1)S(1)}, u32[]{:S(2)}, u32[]{:S(2)}) collective-permute-start(bf16[128,128]{1,0:T(8,128)(2,1)S(1)} %get-tuple-element.61), channel_id=1, source_target_pairs={{0,160},{1,161},{2,162},{3,163},{4,164},{5,165},{6,166},{7,167},{8... | collective-permute-start | bytes 98312 | tf_op jit(solution)/shard_map/ppermute | solution.py:40
  (4 other events, 40.9 us)

commit v2 on v1

--- a/solution.py
+++ b/solution.py
@@ -86,8 +86,10 @@
     return jnp.where(slots < rank, probe, 0.0).astype(BF16)
 
 
-def sketch_kernel(ranks, v_hbm, u_hbm, sketch_hbm, send_ref, keep_ref, v_ref, u_ref, sketch_ref, sems):
-    x, core = place()
+def sketch_kernel(ranks_hbm, v_hbm, u_hbm, sketch_hbm, send_ref, keep_ref, ranks, v_ref, u_ref, sketch_ref, sems):
+    x, core = place()
+    few = pltpu.make_async_copy(ranks_hbm, ranks, sems.at[2 * NU + 1])
+    few.start()
     order = [(k, other) for k in range(NX) for other in (1, 0)]
     tiles = [((x + k) & 3) + 4 * (core ^ other) for k, other in order]
     first = pltpu.make_async_copy(sketch_hbm, sketch_ref, sems.at[2 * NU])
@@ -102,6 +104,7 @@
             copy.start()
         copies.append(pair)
     first.wait()
+    few.wait()
     for i, (k, other) in enumerate(order):
         copies[i][0].wait()
         probe = masked(dot(v_ref[i], sketch_ref[...], NEAR), ranks[tiles[i]])
@@ -120,17 +123,18 @@
     return pl.pallas_call(
         sketch_kernel,
         out_shape=[pltpu.VMEM(out, BF16), pltpu.VMEM(out, F32)],
-        in_specs=[pl.BlockSpec(memory_space=pltpu.SMEM)] + [hbm] * 3,
+        in_specs=[hbm] * 4,
         out_specs=[vmem] * 2,
         scratch_shapes=[
+            pltpu.SMEM(ranks.shape, jnp.int32),
             pltpu.VMEM(v.shape, BF16),
             pltpu.VMEM(u.shape, BF16),
             pltpu.VMEM(sketch.shape, BF16),
-            pltpu.SemaphoreType.DMA((2 * NU + 1,)),
+            pltpu.SemaphoreType.DMA((2 * NU + 2,)),
         ],
         compiler_params=pltpu.CompilerParams(vmem_limit_bytes=16 * 1024 * 1024),
         name="sketch_product",
-    )(ranks, *[pltpu.with_memory_space_constraint(x, pltpu.HBM) for x in (v, u, sketch)])
+    )(*[pltpu.with_memory_space_constraint(x, pltpu.HBM) for x in (ranks, v, u, sketch)])
 
 
 def project_kernel(ranks, u_ref, v_ref, *refs):

time: 128 us -> 126 us (0.984)
  no operation moved by 1% of the time
where the time goes in v2:
time: 126 us
  waiting for transfers between devices  52 us (41%)
  starting transfers between devices  47.6 us (38%)
  Pallas kernels  25.9 us (21%)
    ppermute x29, waiting for transfers between devices, perm(): return lax.ppermute(block, AXES, pairs)  52 us
    ppermute x29, starting transfers between devices, perm(): return lax.ppermute(block, AXES, pairs)  47.6 us
    pallas_call x14, Pallas kernels, call(): pl.pallas_call(kernel, out_shape=shapes, in_specs=[pl.BlockSpec(memory_sp...  20 us
    pallas_call x1, Pallas kernels, sketch_call(): pl.pallas_call(sketch_kernel, out_shape=[pltpu.VMEM(out, BF16), pltpu.VME...  5.06 us
  transfers between devices with their start and end apart: 29, of which 14 were waited for; matrix products, arithmetic and copies ran while one was open for 0% of the time, Pallas kernels for 11%

profile of v2, /device:TPU:1, one launch (start us, length us, event | category | flops | bytes accessed | tf_op | source)
XLA Modules:
  0.0 126.3 jit_solution(12220691761326768103)
XLA Ops:
  0.6 5.1 %sketch_product.1 = (bf16[4,64,1024]{2,1,0:T(8,128)(2,1)S(1)}, f32[4,64,1024]{2,1,0:T(8,128)S(1)}) custom-call(s32[8]{0:T(128)} %bitcast.18, bf16[8,96,1024]{2,1,0:T(8,128)(2,1)} %bitcast.13, bf16[8,96,1024]{2,1,0:T(8,128)(2,1)} %bitcast.15, bf16[64,1024]{1,0:T(8,128)(2,1)} %bitcast.22), custom_call_target="tpu_custom_call" | custom-call | tf_op jit(solution)/shard_map/sketch_product/pallas_call | solution.py:123
  5.7 3.3 %collective-permute-start = (bf16[4,64,1024]{2,1,0:T(8,128)(2,1)S(1)}, bf16[4,64,1024]{2,1,0:T(8,128)(2,1)S(1)}, u32[]{:S(2)}, u32[]{:S(2)}) collective-permute-start(bf16[4,64,1024]{2,1,0:T(8,128)(2,1)S(1)} %get-tuple-element.33), channel_id=1, source_target_pairs={{0,32},{1,33},{2,34},{3,35},{4,36},{5,37},{6,38},{7,39},{8,40},{9,... | collective-permute-start | bytes 1572872 | tf_op jit(solution)/shard_map/ppermute | solution.py:40
  9.3 1.2 collective-permute-done.got_ref
  10.7 1.9 %collective-permute-start.2 = (bf16[64,1024]{1,0:T(8,128)(2,1)S(1)}, bf16[64,1024]{1,0:T(8,128)(2,1)S(1)}, u32[]{:S(2)}, u32[]{:S(2)}) collective-permute-start(bf16[64,1024]{1,0:T(8,128)(2,1)S(1)} %get-tuple-element.36), channel_id=1, source_target_pairs={{0,128},{1,129},{2,130},{3,131},{4,132},{5,133},{6,134},{7,135},{8... | collective-permute-start | bytes 393224 | tf_op jit(solution)/shard_map/ppermute | solution.py:40
  12.7 1.2 collective-permute-start.3
  13.8 3.5 %collective-permute-done.1.a_ref = bf16[64,1024]{1,0:T(8,128)(2,1)S(1)} collective-permute-done((bf16[64,1024]{1,0:T(8,128)(2,1)S(1)}, bf16[64,1024]{1,0:T(8,128)(2,1)S(1)}, u32[]{:S(2)}, u32[]{:S(2)}) %collective-permute-start.1) | collective-permute-done | bytes 131104 | tf_op jit(solution)/shard_map/ppermute | solution.py:40
  17.3 1.4 %collective-permute-done.2.b_ref = bf16[64,1024]{1,0:T(8,128)(2,1)S(1)} collective-permute-done((bf16[64,1024]{1,0:T(8,128)(2,1)S(1)}, bf16[64,1024]{1,0:T(8,128)(2,1)S(1)}, u32[]{:S(2)}, u32[]{:S(2)}) %collective-permute-start.2) | collective-permute-done | bytes 131104 | tf_op jit(solution)/shard_map/ppermute | solution.py:40
  19.8 3.5 %collective-permute-start.6 = (bf16[64,1024]{1,0:T(8,128)(2,1)S(1)}, bf16[64,1024]{1,0:T(8,128)(2,1)S(1)}, u32[]{:S(2)}, u32[]{:S(2)}) collective-permute-start(bf16[64,1024]{1,0:T(8,128)(2,1)S(1)} %shard_map.87.a_ref.summed_ref.refs_0_.sum_ref), channel_id=1, source_target_pairs={{0,192},{1,193},{2,194},{3,195},{4,196},{5,197},{6,198},{7,199},{8... | collective-permute-start | bytes 393224 | tf_op jit(solution)/shard_map/ppermute | solution.py:40
  24.0 4.6 %collective-permute-done.6.d_ref.refs_3_ = bf16[64,1024]{1,0:T(8,128)(2,1)S(1)} collective-permute-done((bf16[64,1024]{1,0:T(8,128)(2,1)S(1)}, bf16[64,1024]{1,0:T(8,128)(2,1)S(1)}, u32[]{:S(2)}, u32[]{:S(2)}) %collective-permute-start.6) | collective-permute-done | bytes 131104 | tf_op jit(solution)/shard_map/ppermute | solution.py:40
  29.1 3.3 %collective-permute-done.4.b_ref.refs_1_ = bf16[64,1024]{1,0:T(8,128)(2,1)S(1)} collective-permute-done((bf16[64,1024]{1,0:T(8,128)(2,1)S(1)}, bf16[64,1024]{1,0:T(8,128)(2,1)S(1)}, u32[]{:S(2)}, u32[]{:S(2)}) %collective-permute-start.4) | collective-permute-done | bytes 131104 | tf_op jit(solution)/shard_map/ppermute | solution.py:40
  33.3 1.5 %collective-permute-done.7.refs_4_ = bf16[4,64,1024]{2,1,0:T(8,128)(2,1)S(1)} collective-permute-done((bf16[4,64,1024]{2,1,0:T(8,128)(2,1)S(1)}, bf16[4,64,1024]{2,1,0:T(8,128)(2,1)S(1)}, u32[]{:S(2)}, u32[]{:S(2)}) %collective-permute-start.7) | collective-permute-done | bytes 524320 | tf_op jit(solution)/shard_map/ppermute | solution.py:40
  34.9 3.1 %shard_map.90 = (bf16[4,64,1024]{2,1,0:T(8,128)(2,1)S(1)}, f32[4,64,1024]{2,1,0:T(8,128)S(1)}) custom-call(s32[8]{0:T(128)S(1)} %bitcast.19, bf16[8,96,1024]{2,1,0:T(8,128)(2,1)S(1)} %bitcast.16, bf16[8,96,1024]{2,1,0:T(8,128)(2,1)S(1)} %bitcast.14, bf16[64,1024]{1,0:T(8,128)(2,1)S(1)} %shard_map.87.a_ref.summed_ref.refs_0_.sum_ref, ...), custom_call_target="tpu_custom_call" | custom-call | tf_op jit(solution)/shard_map/pallas_call | solution.py:74
  38.6 1.8 %collective-permute-start.14 = (bf16[2,128,1024]{2,1,0:T(8,128)(2,1)S(1)}, bf16[2,128,1024]{2,1,0:T(8,128)(2,1)S(1)}, u32[]{:S(2)}, u32[]{:S(2)}) collective-permute-start(bf16[2,128,1024]{2,1,0:T(8,128)(2,1)S(1)} %get-tuple-element.47), channel_id=1, source_target_pairs={{0,128},{1,129},{2,130},{3,131},{4,132},{5,133},{6,134},{7,135},{8... | collective-permute-start | bytes 1572872 | tf_op jit(solution)/shard_map/ppermute | solution.py:40
  42.2 1.9 %collective-permute-start.10 = (bf16[64,1024]{1,0:T(8,128)(2,1)S(1)}, bf16[64,1024]{1,0:T(8,128)(2,1)S(1)}, u32[]{:S(2)}, u32[]{:S(2)}) collective-permute-start(bf16[64,1024]{1,0:T(8,128)(2,1)S(1)} %get-tuple-element.42), channel_id=1, source_target_pairs={{0,128},{1,129},{2,130},{3,131},{4,132},{5,133},{6,134},{7,135},{8... | collective-permute-start | bytes 393224 | tf_op jit(solution)/shard_map/ppermute | solution.py:40
  44.1 19.9 %collective-permute-done.13.refs_2_ = bf16[2,128,1024]{2,1,0:T(8,128)(2,1)S(1)} collective-permute-done((bf16[2,128,1024]{2,1,0:T(8,128)(2,1)S(1)}, bf16[2,128,1024]{2,1,0:T(8,128)(2,1)S(1)}, u32[]{:S(2)}, u32[]{:S(2)}) %collective-permute-start.13) | collective-permute-done | bytes 524320 | tf_op jit(solution)/shard_map/ppermute | solution.py:40
  64.1 6.1 %shard_map.89.inverse_ref = f32[64,64]{1,0:T(8,128)S(1)} custom-call(bf16[64,1024]{1,0:T(8,128)(2,1)S(1)} %shard_map.87.a_ref.summed_ref.refs_0_.sum_ref), custom_call_target="tpu_custom_call" | custom-call | tf_op jit(solution)/shard_map/pallas_call | solution.py:74
  70.4 5.6 %shard_map.94 = (bf16[64,1024]{1,0:T(8,128)(2,1)S(1)}, bf16[2,128,640]{2,1,0:T(8,128)(2,1)S(1)}, bf16[2,128,640]{2,1,0:T(8,128)(2,1)S(1)}, bf16[2,128,640]{2,1,0:T(8,128)(2,1)S(1)}, bf16[2,128,640]{2,1,0:T(8,128)(2,1)S(1)}) custom-call(bf16[64,1024]{1,0:T(8,128)(2,1)S(1)} %shard_map.87.a_ref.summed_ref.refs_0_.sum_ref, f32[64,64]{1,0:T(8,128)S(1)} %shard_map.89.inverse_ref, ...), custom_call_target="tpu_custom_call" | custom-call | tf_op jit(solution)/shard_map/pallas_call | solution.py:74
  76.0 2.7 %collective-permute-start.20 = (bf16[2,128,640]{2,1,0:T(8,128)(2,1)S(1)}, bf16[2,128,640]{2,1,0:T(8,128)(2,1)S(1)}, u32[]{:S(2)}, u32[]{:S(2)}) collective-permute-start(bf16[2,128,640]{2,1,0:T(8,128)(2,1)S(1)} %get-tuple-element.50), channel_id=1, source_target_pairs={{0,1},{1,2},{2,3},{3,0},{4,5},{5,6},{6,7},{7,4},{8,9},{9,10},{10,1... | collective-permute-start | bytes 983048 | tf_op jit(solution)/shard_map/ppermute | solution.py:40
  78.7 4.6 %collective-permute-start.21 = (bf16[2,128,640]{2,1,0:T(8,128)(2,1)S(1)}, bf16[2,128,640]{2,1,0:T(8,128)(2,1)S(1)}, u32[]{:S(2)}, u32[]{:S(2)}) collective-permute-start(bf16[2,128,640]{2,1,0:T(8,128)(2,1)S(1)} %get-tuple-element.51), channel_id=1, source_target_pairs={{0,65},{1,66},{2,67},{3,64},{4,69},{5,70},{6,71},{7,68},{8,73},{9,... | collective-permute-start | bytes 983048 | tf_op jit(solution)/shard_map/ppermute | solution.py:40
  83.3 1.9 %collective-permute-start.22 = (bf16[2,128,640]{2,1,0:T(8,128)(2,1)S(1)}, bf16[2,128,640]{2,1,0:T(8,128)(2,1)S(1)}, u32[]{:S(2)}, u32[]{:S(2)}) collective-permute-start(bf16[2,128,640]{2,1,0:T(8,128)(2,1)S(1)} %get-tuple-element.52), channel_id=1, source_target_pairs={{0,129},{1,130},{2,131},{3,128},{4,133},{5,134},{6,135},{7,132},{8... | collective-permute-start | bytes 983048 | tf_op jit(solution)/shard_map/ppermute | solution.py:40
  85.2 3.5 %collective-permute-start.23 = (bf16[2,128,640]{2,1,0:T(8,128)(2,1)S(1)}, bf16[2,128,640]{2,1,0:T(8,128)(2,1)S(1)}, u32[]{:S(2)}, u32[]{:S(2)}) collective-permute-start(bf16[2,128,640]{2,1,0:T(8,128)(2,1)S(1)} %get-tuple-element.53), channel_id=1, source_target_pairs={{0,193},{1,194},{2,195},{3,192},{4,197},{5,198},{6,199},{7,196},{8... | collective-permute-start | bytes 983048 | tf_op jit(solution)/shard_map/ppermute | solution.py:40
  88.7 3.8 %collective-permute-start.18 = (bf16[64,1024]{1,0:T(8,128)(2,1)S(1)}, bf16[64,1024]{1,0:T(8,128)(2,1)S(1)}, u32[]{:S(2)}, u32[]{:S(2)}) collective-permute-start(bf16[64,1024]{1,0:T(8,128)(2,1)S(1)} %get-tuple-element.49.a_ref.refs_5_), channel_id=1, source_target_pairs={{0,192},{1,193},{2,194},{3,195},{4,196},{5,197},{6,198},{7,199},{8... | collective-permute-start | bytes 393224 | tf_op jit(solution)/shard_map/ppermute | solution.py:40
  92.5 1.2 collective-permute-start.17
  93.7 2.1 %collective-permute-start.16 = (bf16[64,1024]{1,0:T(8,128)(2,1)S(1)}, bf16[64,1024]{1,0:T(8,128)(2,1)S(1)}, u32[]{:S(2)}, u32[]{:S(2)}) collective-permute-start(bf16[64,1024]{1,0:T(8,128)(2,1)S(1)} %get-tuple-element.49.a_ref.refs_5_), channel_id=1, source_target_pairs={{0,64},{1,65},{2,66},{3,67},{4,68},{5,69},{6,70},{7,71},{8,72},{9,... | collective-permute-start | bytes 393224 | tf_op jit(solution)/shard_map/ppermute | solution.py:40
  95.8 1.2 collective-permute-done.22.c_ref
  97.0 4.6 %collective-permute-done.23.d_ref = bf16[2,128,640]{2,1,0:T(8,128)(2,1)S(1)} collective-permute-done((bf16[2,128,640]{2,1,0:T(8,128)(2,1)S(1)}, bf16[2,128,640]{2,1,0:T(8,128)(2,1)S(1)}, u32[]{:S(2)}, u32[]{:S(2)}) %collective-permute-start.23) | collective-permute-done | bytes 327712 | tf_op jit(solution)/shard_map/ppermute | solution.py:40
  102.0 3.2 %collective-permute-start.24 = (bf16[2,128,640]{2,1,0:T(8,128)(2,1)S(1)}, bf16[2,128,640]{2,1,0:T(8,128)(2,1)S(1)}, u32[]{:S(2)}, u32[]{:S(2)}) collective-permute-start(bf16[2,128,640]{2,1,0:T(8,128)(2,1)S(1)} %get-tuple-element.55), channel_id=1, source_target_pairs={{0,32},{1,33},{2,34},{3,35},{4,36},{5,37},{6,38},{7,39},{8,40},{9,... | collective-permute-start | bytes 983048 | tf_op jit(solution)/shard_map/ppermute | solution.py:40
  105.3 1.2 collective-permute-start.19
  106.6 2.1 %collective-permute-start.25 = (bf16[128,640]{1,0:T(8,128)(2,1)S(1)}, bf16[128,640]{1,0:T(8,128)(2,1)S(1)}, u32[]{:S(2)}, u32[]{:S(2)}) collective-permute-start(bf16[128,640]{1,0:T(8,128)(2,1)S(1)} %get-tuple-element.57), channel_id=1, source_target_pairs={{0,4},{1,5},{2,6},{3,7},{4,8},{5,9},{6,10},{7,11},{8,12},{9,13},{1... | collective-permute-start | bytes 491528 | tf_op jit(solution)/shard_map/ppermute | solution.py:40
  108.7 8.2 %collective-permute-done.25.onward_ref = bf16[128,640]{1,0:T(8,128)(2,1)S(1)} collective-permute-done((bf16[128,640]{1,0:T(8,128)(2,1)S(1)}, bf16[128,640]{1,0:T(8,128)(2,1)S(1)}, u32[]{:S(2)}, u32[]{:S(2)}) %collective-permute-start.25) | collective-permute-done | bytes 163872 | tf_op jit(solution)/shard_map/ppermute | solution.py:40
  117.6 3.0 %collective-permute-start.27 = (bf16[128,128]{1,0:T(8,128)(2,1)S(1)}, bf16[128,128]{1,0:T(8,128)(2,1)S(1)}, u32[]{:S(2)}, u32[]{:S(2)}) collective-permute-start(bf16[128,128]{1,0:T(8,128)(2,1)S(1)} %get-tuple-element.60), channel_id=1, source_target_pairs={{0,192},{1,193},{2,194},{3,195},{4,196},{5,197},{6,198},{7,199},{8... | collective-permute-start | bytes 98312 | tf_op jit(solution)/shard_map/ppermute | solution.py:40
  120.8 4.0 %shard_map.96 = bf16[8,128,1024]{2,1,0:T(8,128)(2,1)} custom-call(bf16[8,128,1024]{2,1,0:T(8,128)(2,1)S(1)} %bitcast.12, bf16[1024,1024]{1,0:T(8,128)(2,1)S(1)} %bitcast.10, bf16[64,1024]{1,0:T(8,128)(2,1)S(1)} %shard_map.87.a_ref.summed_ref.refs_0_.sum_ref, bf16[64,1024]{1,0:T(8,128)(2,1)S(1)} %collective-permute-done.4.b_ref.refs_1_, ...), custom_call_target="tpu_custom_call" | custom-call | tf_op jit(solution)/shard_map/pallas_call | solution.py:74
  (54 shorter events, 9.4 us)
Async XLA Ops:
  5.7 4.8 %collective-permute-start = (bf16[4,64,1024]{2,1,0:T(8,128)(2,1)S(1)}, bf16[4,64,1024]{2,1,0:T(8,128)(2,1)S(1)}, u32[]{:S(2)}, u32[]{:S(2)}) collective-permute-start(bf16[4,64,1024]{2,1,0:T(8,128)(2,1)S(1)} %get-tuple-element.33), channel_id=1, source_target_pairs={{0,32},{1,33},{2,34},{3,35},{4,36},{5,37},{6,38},{7,39},{8,40},{9,... | collective-permute-start | bytes 1572872 | tf_op jit(solution)/shard_map/ppermute | solution.py:40
  9.1 25.7 %copy-start.2 = (bf16[1,8,1,96,1024]{4,3,2,1,0:T(8,128)(2,1)S(1)}, bf16[1,8,1,96,1024]{4,3,2,1,0:T(8,128)(2,1)}, u32[]{:S(2)}) copy-start(bf16[1,8,1,96,1024]{4,3,2,1,0:T(8,128)(2,1)} %param.11) | copy-start | bytes 4718596
  9.1 25.7 %copy-start.3 = (bf16[1,8,1,96,1024]{4,3,2,1,0:T(8,128)(2,1)S(1)}, bf16[1,8,1,96,1024]{4,3,2,1,0:T(8,128)(2,1)}, u32[]{:S(2)}) copy-start(bf16[1,8,1,96,1024]{4,3,2,1,0:T(8,128)(2,1)} %param.10) | copy-start | bytes 4718596
  9.2 29.3 %collective-permute-start.12 = (bf16[4,128,1024]{2,1,0:T(8,128)(2,1)S(1)}, bf16[4,128,1024]{2,1,0:T(8,128)(2,1)S(1)}, u32[]{:S(2)}, u32[]{:S(2)}) collective-permute-start(bf16[4,128,1024]{2,1,0:T(8,128)(2,1)S(1)} %get-tuple-element.45), channel_id=1, source_target_pairs={{0,32},{1,33},{2,34},{3,35},{4,36},{5,37},{6,38},{7,39},{8,40},{9,... | collective-permute-start | bytes 3145736 | tf_op jit(solution)/shard_map/ppermute | solution.py:40
  10.6 6.7 %collective-permute-start.1 = (bf16[64,1024]{1,0:T(8,128)(2,1)S(1)}, bf16[64,1024]{1,0:T(8,128)(2,1)S(1)}, u32[]{:S(2)}, u32[]{:S(2)}) collective-permute-start(bf16[64,1024]{1,0:T(8,128)(2,1)S(1)} %get-tuple-element.35), channel_id=1, source_target_pairs={{0,64},{1,65},{2,66},{3,67},{4,68},{5,69},{6,70},{7,71},{8,72},{9,... | collective-permute-start | bytes 393224 | tf_op jit(solution)/shard_map/ppermute | solution.py:40
  10.7 8.0 %collective-permute-start.2 = (bf16[64,1024]{1,0:T(8,128)(2,1)S(1)}, bf16[64,1024]{1,0:T(8,128)(2,1)S(1)}, u32[]{:S(2)}, u32[]{:S(2)}) collective-permute-start(bf16[64,1024]{1,0:T(8,128)(2,1)S(1)} %get-tuple-element.36), channel_id=1, source_target_pairs={{0,128},{1,129},{2,130},{3,131},{4,132},{5,133},{6,134},{7,135},{8... | collective-permute-start | bytes 393224 | tf_op jit(solution)/shard_map/ppermute | solution.py:40
  12.7 7.1 %collective-permute-start.3 = (bf16[64,1024]{1,0:T(8,128)(2,1)S(1)}, bf16[64,1024]{1,0:T(8,128)(2,1)S(1)}, u32[]{:S(2)}, u32[]{:S(2)}) collective-permute-start(bf16[64,1024]{1,0:T(8,128)(2,1)S(1)} %get-tuple-element.37), channel_id=1, source_target_pairs={{0,192},{1,193},{2,194},{3,195},{4,196},{5,197},{6,198},{7,199},{8... | collective-permute-start | bytes 393224 | tf_op jit(solution)/shard_map/ppermute | solution.py:40
  19.8 8.8 %collective-permute-start.6 = (bf16[64,1024]{1,0:T(8,128)(2,1)S(1)}, bf16[64,1024]{1,0:T(8,128)(2,1)S(1)}, u32[]{:S(2)}, u32[]{:S(2)}) collective-permute-start(bf16[64,1024]{1,0:T(8,128)(2,1)S(1)} %shard_map.87.a_ref.summed_ref.refs_0_.sum_ref), channel_id=1, source_target_pairs={{0,192},{1,193},{2,194},{3,195},{4,196},{5,197},{6,198},{7,199},{8... | collective-permute-start | bytes 393224 | tf_op jit(solution)/shard_map/ppermute | solution.py:40
  23.3 5.9 %collective-permute-start.5 = (bf16[64,1024]{1,0:T(8,128)(2,1)S(1)}, bf16[64,1024]{1,0:T(8,128)(2,1)S(1)}, u32[]{:S(2)}, u32[]{:S(2)}) collective-permute-start(bf16[64,1024]{1,0:T(8,128)(2,1)S(1)} %shard_map.87.a_ref.summed_ref.refs_0_.sum_ref), channel_id=1, source_target_pairs={{0,128},{1,129},{2,130},{3,131},{4,132},{5,133},{6,134},{7,135},{8... | collective-permute-start | bytes 393224 | tf_op jit(solution)/shard_map/ppermute | solution.py:40
  23.3 9.1 %collective-permute-start.4 = (bf16[64,1024]{1,0:T(8,128)(2,1)S(1)}, bf16[64,1024]{1,0:T(8,128)(2,1)S(1)}, u32[]{:S(2)}, u32[]{:S(2)}) collective-permute-start(bf16[64,1024]{1,0:T(8,128)(2,1)S(1)} %shard_map.87.a_ref.summed_ref.refs_0_.sum_ref), channel_id=1, source_target_pairs={{0,64},{1,65},{2,66},{3,67},{4,68},{5,69},{6,70},{7,71},{8,72},{9,... | collective-permute-start | bytes 393224 | tf_op jit(solution)/shard_map/ppermute | solution.py:40
  32.5 2.4 %collective-permute-start.7 = (bf16[4,64,1024]{2,1,0:T(8,128)(2,1)S(1)}, bf16[4,64,1024]{2,1,0:T(8,128)(2,1)S(1)}, u32[]{:S(2)}, u32[]{:S(2)}) collective-permute-start(bf16[4,64,1024]{2,1,0:T(8,128)(2,1)S(1)} %shard_map.88), channel_id=1, source_target_pairs={{0,32},{1,33},{2,34},{3,35},{4,36},{5,37},{6,38},{7,39},{8,40},{9,... | collective-permute-start | bytes 1572872 | tf_op jit(solution)/shard_map/ppermute | solution.py:40
  38.0 32.5 %copy-start = (bf16[1,1024,1024]{2,1,0:T(8,128)(2,1)S(1)}, bf16[1,1024,1024]{2,1,0:T(8,128)(2,1)}, u32[]{:S(2)}) copy-start(bf16[1,1024,1024]{2,1,0:T(8,128)(2,1)} %param.9) | copy-start | bytes 6291460
  38.0 3.3 %collective-permute-start.8 = (bf16[4,64,1024]{2,1,0:T(8,128)(2,1)S(1)}, bf16[4,64,1024]{2,1,0:T(8,128)(2,1)S(1)}, u32[]{:S(2)}, u32[]{:S(2)}) collective-permute-start(bf16[4,64,1024]{2,1,0:T(8,128)(2,1)S(1)} %get-tuple-element.39), channel_id=1, source_target_pairs={{0,32},{1,33},{2,34},{3,35},{4,36},{5,37},{6,38},{7,39},{8,40},{9,... | collective-permute-start | bytes 1572872 | tf_op jit(solution)/shard_map/ppermute | solution.py:40
  38.5 25.5 %collective-permute-start.13 = (bf16[2,128,1024]{2,1,0:T(8,128)(2,1)S(1)}, bf16[2,128,1024]{2,1,0:T(8,128)(2,1)S(1)}, u32[]{:S(2)}, u32[]{:S(2)}) collective-permute-start(bf16[2,128,1024]{2,1,0:T(8,128)(2,1)S(1)} %get-tuple-element.46), channel_id=1, source_target_pairs={{0,64},{1,65},{2,66},{3,67},{4,68},{5,69},{6,70},{7,71},{8,72},{9,... | collective-permute-start | bytes 1572872 | tf_op jit(solution)/shard_map/ppermute | solution.py:40
  38.6 31.5 %collective-permute-start.14 = (bf16[2,128,1024]{2,1,0:T(8,128)(2,1)S(1)}, bf16[2,128,1024]{2,1,0:T(8,128)(2,1)S(1)}, u32[]{:S(2)}, u32[]{:S(2)}) collective-permute-start(bf16[2,128,1024]{2,1,0:T(8,128)(2,1)S(1)} %get-tuple-element.47), channel_id=1, source_target_pairs={{0,128},{1,129},{2,130},{3,131},{4,132},{5,133},{6,134},{7,135},{8... | collective-permute-start | bytes 1572872 | tf_op jit(solution)/shard_map/ppermute | solution.py:40
  40.4 29.7 %collective-permute-start.15 = (bf16[2,128,1024]{2,1,0:T(8,128)(2,1)S(1)}, bf16[2,128,1024]{2,1,0:T(8,128)(2,1)S(1)}, u32[]{:S(2)}, u32[]{:S(2)}) collective-permute-start(bf16[2,128,1024]{2,1,0:T(8,128)(2,1)S(1)} %get-tuple-element.48), channel_id=1, source_target_pairs={{0,192},{1,193},{2,194},{3,195},{4,196},{5,197},{6,198},{7,199},{8... | collective-permute-start | bytes 1572872 | tf_op jit(solution)/shard_map/ppermute | solution.py:40
  41.4 28.8 %collective-permute-start.9 = (bf16[64,1024]{1,0:T(8,128)(2,1)S(1)}, bf16[64,1024]{1,0:T(8,128)(2,1)S(1)}, u32[]{:S(2)}, u32[]{:S(2)}) collective-permute-start(bf16[64,1024]{1,0:T(8,128)(2,1)S(1)} %get-tuple-element.41), channel_id=1, source_target_pairs={{0,64},{1,65},{2,66},{3,67},{4,68},{5,69},{6,70},{7,71},{8,72},{9,... | collective-permute-start | bytes 393224 | tf_op jit(solution)/shard_map/ppermute | solution.py:40
  42.2 27.9 %collective-permute-start.10 = (bf16[64,1024]{1,0:T(8,128)(2,1)S(1)}, bf16[64,1024]{1,0:T(8,128)(2,1)S(1)}, u32[]{:S(2)}, u32[]{:S(2)}) collective-permute-start(bf16[64,1024]{1,0:T(8,128)(2,1)S(1)} %get-tuple-element.42), channel_id=1, source_target_pairs={{0,128},{1,129},{2,130},{3,131},{4,132},{5,133},{6,134},{7,135},{8... | collective-permute-start | bytes 393224 | tf_op jit(solution)/shard_map/ppermute | solution.py:40
  64.1 6.4 %collective-permute-start.11 = (bf16[64,1024]{1,0:T(8,128)(2,1)S(1)}, bf16[64,1024]{1,0:T(8,128)(2,1)S(1)}, u32[]{:S(2)}, u32[]{:S(2)}) collective-permute-start(bf16[64,1024]{1,0:T(8,128)(2,1)S(1)} %get-tuple-element.43), channel_id=1, source_target_pairs={{0,192},{1,193},{2,194},{3,195},{4,196},{5,197},{6,198},{7,199},{8... | collective-permute-start | bytes 393224 | tf_op jit(solution)/shard_map/ppermute | solution.py:40
  76.0 16.5 %collective-permute-start.20 = (bf16[2,128,640]{2,1,0:T(8,128)(2,1)S(1)}, bf16[2,128,640]{2,1,0:T(8,128)(2,1)S(1)}, u32[]{:S(2)}, u32[]{:S(2)}) collective-permute-start(bf16[2,128,640]{2,1,0:T(8,128)(2,1)S(1)} %get-tuple-element.50), channel_id=1, source_target_pairs={{0,1},{1,2},{2,3},{3,0},{4,5},{5,6},{6,7},{7,4},{8,9},{9,10},{10,1... | collective-permute-start | bytes 983048 | tf_op jit(solution)/shard_map/ppermute | solution.py:40
  78.7 15.0 %collective-permute-start.21 = (bf16[2,128,640]{2,1,0:T(8,128)(2,1)S(1)}, bf16[2,128,640]{2,1,0:T(8,128)(2,1)S(1)}, u32[]{:S(2)}, u32[]{:S(2)}) collective-permute-start(bf16[2,128,640]{2,1,0:T(8,128)(2,1)S(1)} %get-tuple-element.51), channel_id=1, source_target_pairs={{0,65},{1,66},{2,67},{3,64},{4,69},{5,70},{6,71},{7,68},{8,73},{9,... | collective-permute-start | bytes 983048 | tf_op jit(solution)/shard_map/ppermute | solution.py:40
  83.3 13.7 %collective-permute-start.22 = (bf16[2,128,640]{2,1,0:T(8,128)(2,1)S(1)}, bf16[2,128,640]{2,1,0:T(8,128)(2,1)S(1)}, u32[]{:S(2)}, u32[]{:S(2)}) collective-permute-start(bf16[2,128,640]{2,1,0:T(8,128)(2,1)S(1)} %get-tuple-element.52), channel_id=1, source_target_pairs={{0,129},{1,130},{2,131},{3,128},{4,133},{5,134},{6,135},{7,132},{8... | collective-permute-start | bytes 983048 | tf_op jit(solution)/shard_map/ppermute | solution.py:40
  85.2 16.3 %collective-permute-start.23 = (bf16[2,128,640]{2,1,0:T(8,128)(2,1)S(1)}, bf16[2,128,640]{2,1,0:T(8,128)(2,1)S(1)}, u32[]{:S(2)}, u32[]{:S(2)}) collective-permute-start(bf16[2,128,640]{2,1,0:T(8,128)(2,1)S(1)} %get-tuple-element.53), channel_id=1, source_target_pairs={{0,193},{1,194},{2,195},{3,192},{4,197},{5,198},{6,199},{7,196},{8... | collective-permute-start | bytes 983048 | tf_op jit(solution)/shard_map/ppermute | solution.py:40
  88.7 16.6 %collective-permute-start.18 = (bf16[64,1024]{1,0:T(8,128)(2,1)S(1)}, bf16[64,1024]{1,0:T(8,128)(2,1)S(1)}, u32[]{:S(2)}, u32[]{:S(2)}) collective-permute-start(bf16[64,1024]{1,0:T(8,128)(2,1)S(1)} %get-tuple-element.49.a_ref.refs_5_), channel_id=1, source_target_pairs={{0,192},{1,193},{2,194},{3,195},{4,196},{5,197},{6,198},{7,199},{8... | collective-permute-start | bytes 393224 | tf_op jit(solution)/shard_map/ppermute | solution.py:40
  92.5 12.8 %collective-permute-start.17 = (bf16[64,1024]{1,0:T(8,128)(2,1)S(1)}, bf16[64,1024]{1,0:T(8,128)(2,1)S(1)}, u32[]{:S(2)}, u32[]{:S(2)}) collective-permute-start(bf16[64,1024]{1,0:T(8,128)(2,1)S(1)} %get-tuple-element.49.a_ref.refs_5_), channel_id=1, source_target_pairs={{0,128},{1,129},{2,130},{3,131},{4,132},{5,133},{6,134},{7,135},{8... | collective-permute-start | bytes 393224 | tf_op jit(solution)/shard_map/ppermute | solution.py:40
  93.7 11.6 %collective-permute-start.16 = (bf16[64,1024]{1,0:T(8,128)(2,1)S(1)}, bf16[64,1024]{1,0:T(8,128)(2,1)S(1)}, u32[]{:S(2)}, u32[]{:S(2)}) collective-permute-start(bf16[64,1024]{1,0:T(8,128)(2,1)S(1)} %get-tuple-element.49.a_ref.refs_5_), channel_id=1, source_target_pairs={{0,64},{1,65},{2,66},{3,67},{4,68},{5,69},{6,70},{7,71},{8,72},{9,... | collective-permute-start | bytes 393224 | tf_op jit(solution)/shard_map/ppermute | solution.py:40
  102.0 4.5 %collective-permute-start.24 = (bf16[2,128,640]{2,1,0:T(8,128)(2,1)S(1)}, bf16[2,128,640]{2,1,0:T(8,128)(2,1)S(1)}, u32[]{:S(2)}, u32[]{:S(2)}) collective-permute-start(bf16[2,128,640]{2,1,0:T(8,128)(2,1)S(1)} %get-tuple-element.55), channel_id=1, source_target_pairs={{0,32},{1,33},{2,34},{3,35},{4,36},{5,37},{6,38},{7,39},{8,40},{9,... | collective-permute-start | bytes 983048 | tf_op jit(solution)/shard_map/ppermute | solution.py:40
  105.3 15.4 %collective-permute-start.19 = (bf16[4,64,1024]{2,1,0:T(8,128)(2,1)S(1)}, bf16[4,64,1024]{2,1,0:T(8,128)(2,1)S(1)}, u32[]{:S(2)}, u32[]{:S(2)}) collective-permute-start(bf16[4,64,1024]{2,1,0:T(8,128)(2,1)S(1)} %shard_map.95), channel_id=1, source_target_pairs={{0,32},{1,33},{2,34},{3,35},{4,36},{5,37},{6,38},{7,39},{8,40},{9,... | collective-permute-start | bytes 1572872 | tf_op jit(solution)/shard_map/ppermute | solution.py:40
  106.6 10.3 %collective-permute-start.25 = (bf16[128,640]{1,0:T(8,128)(2,1)S(1)}, bf16[128,640]{1,0:T(8,128)(2,1)S(1)}, u32[]{:S(2)}, u32[]{:S(2)}) collective-permute-start(bf16[128,640]{1,0:T(8,128)(2,1)S(1)} %get-tuple-element.57), channel_id=1, source_target_pairs={{0,4},{1,5},{2,6},{3,7},{4,8},{5,9},{6,10},{7,11},{8,12},{9,13},{1... | collective-permute-start | bytes 491528 | tf_op jit(solution)/shard_map/ppermute | solution.py:40
  117.0 7.8 %collective-permute-start.26 = (bf16[128,128]{1,0:T(8,128)(2,1)S(1)}, bf16[128,128]{1,0:T(8,128)(2,1)S(1)}, u32[]{:S(2)}, u32[]{:S(2)}) collective-permute-start(bf16[128,128]{1,0:T(8,128)(2,1)S(1)} %get-tuple-element.59), channel_id=1, source_target_pairs={{0,224},{1,225},{2,226},{3,227},{4,228},{5,229},{6,230},{7,231},{8... | collective-permute-start | bytes 98312 | tf_op jit(solution)/shard_map/ppermute | solution.py:40
  117.6 7.2 %collective-permute-start.27 = (bf16[128,128]{1,0:T(8,128)(2,1)S(1)}, bf16[128,128]{1,0:T(8,128)(2,1)S(1)}, u32[]{:S(2)}, u32[]{:S(2)}) collective-permute-start(bf16[128,128]{1,0:T(8,128)(2,1)S(1)} %get-tuple-element.60), channel_id=1, source_target_pairs={{0,192},{1,193},{2,194},{3,195},{4,196},{5,197},{6,198},{7,199},{8... | collective-permute-start | bytes 98312 | tf_op jit(solution)/shard_map/ppermute | solution.py:40
  120.6 4.8 %collective-permute-start.28 = (bf16[128,128]{1,0:T(8,128)(2,1)S(1)}, bf16[128,128]{1,0:T(8,128)(2,1)S(1)}, u32[]{:S(2)}, u32[]{:S(2)}) collective-permute-start(bf16[128,128]{1,0:T(8,128)(2,1)S(1)} %get-tuple-element.61), channel_id=1, source_target_pairs={{0,160},{1,161},{2,162},{3,163},{4,164},{5,165},{6,166},{7,167},{8... | collective-permute-start | bytes 98312 | tf_op jit(solution)/shard_map/ppermute | solution.py:40
  (3 other events, 38.9 us)

commit v3 on v2

--- a/solution.py
+++ b/solution.py
@@ -133,7 +133,6 @@
             pltpu.SemaphoreType.DMA((2 * NU + 2,)),
         ],
         compiler_params=pltpu.CompilerParams(vmem_limit_bytes=16 * 1024 * 1024),
-        name="sketch_product",
     )(*[pltpu.with_memory_space_constraint(x, pltpu.HBM) for x in (ranks, v, u, sketch)])
 
 
@@ -271,9 +270,7 @@
 def tile_call(summed, inverse, parts, dinv, rows):
     width = dinv.shape[0]
     out = ((2, BLK, HALF * BLK), BF16)
-    return call(
-        tile_kernel,
-        [(summed.shape, BF16)] + [out] * NX,
+    return call(tile_kernel, [(summed.shape, BF16)] + [out] * NX,
         [summed, inverse, *parts, dinv, *rows],
         scratch=[
             pltpu.VMEM((NX, 2 * BLK, width), BF16),
@@ -308,9 +305,7 @@
 
 
 def rows_call(panel, dinv, bases, crosses):
-    return call(
-        rows_kernel,
-        [(panel.shape, BF16)],
+    return call(rows_kernel, [(panel.shape, BF16)],
         [panel, dinv, *bases, *crosses],
         scratch=[
             pltpu.VMEM((2 * BLK, panel.shape[2]), BF16),
@@ -390,7 +385,6 @@
         in_specs=[vmem] * len(ins),
         out_specs=vmem,
         compiler_params=pltpu.CompilerParams(vmem_limit_bytes=16 * 1024 * 1024),
-        name="diagonal",
     )(*[pltpu.with_memory_space_constraint(x, pltpu.VMEM) for x in ins])
 
 

time: 126 us -> 126 us (level)
  no operation moved by 1% of the time
where the time goes in v3:
time: 126 us
  waiting for transfers between devices  52 us (41%)
  starting transfers between devices  47.6 us (38%)
  Pallas kernels  25.9 us (21%)
    ppermute x29, waiting for transfers between devices, perm(): return lax.ppermute(block, AXES, pairs)  52 us
    ppermute x29, starting transfers between devices, perm(): return lax.ppermute(block, AXES, pairs)  47.6 us
    pallas_call x14, Pallas kernels, call(): pl.pallas_call(kernel, out_shape=shapes, in_specs=[pl.BlockSpec(memory_sp...  20 us
    pallas_call x1, Pallas kernels, sketch_call(): pl.pallas_call(sketch_kernel, out_shape=[pltpu.VMEM(out, BF16), pltpu.VME...  5.06 us
  transfers between devices with their start and end apart: 29, of which 14 were waited for; matrix products, arithmetic and copies ran while one was open for 0% of the time, Pallas kernels for 11%

profile of v3, /device:TPU:1, one launch (start us, length us, event | category | flops | bytes accessed | tf_op | source)
XLA Modules:
  0.0 126.3 jit_solution(12220691761326768103)
XLA Ops:
  0.6 5.1 %shard_map.86 = (bf16[4,64,1024]{2,1,0:T(8,128)(2,1)S(1)}, f32[4,64,1024]{2,1,0:T(8,128)S(1)}) custom-call(s32[8]{0:T(128)} %bitcast.18, bf16[8,96,1024]{2,1,0:T(8,128)(2,1)} %bitcast.13, bf16[8,96,1024]{2,1,0:T(8,128)(2,1)} %bitcast.15, bf16[64,1024]{1,0:T(8,128)(2,1)} %bitcast.22), custom_call_target="tpu_custom_call" | custom-call | tf_op jit(solution)/shard_map/pallas_call | solution.py:123
  5.7 3.3 %collective-permute-start = (bf16[4,64,1024]{2,1,0:T(8,128)(2,1)S(1)}, bf16[4,64,1024]{2,1,0:T(8,128)(2,1)S(1)}, u32[]{:S(2)}, u32[]{:S(2)}) collective-permute-start(bf16[4,64,1024]{2,1,0:T(8,128)(2,1)S(1)} %get-tuple-element.33), channel_id=1, source_target_pairs={{0,32},{1,33},{2,34},{3,35},{4,36},{5,37},{6,38},{7,39},{8,40},{9,... | collective-permute-start | bytes 1572872 | tf_op jit(solution)/shard_map/ppermute | solution.py:40
  9.3 1.2 collective-permute-done.got_ref
  10.7 1.9 %collective-permute-start.2 = (bf16[64,1024]{1,0:T(8,128)(2,1)S(1)}, bf16[64,1024]{1,0:T(8,128)(2,1)S(1)}, u32[]{:S(2)}, u32[]{:S(2)}) collective-permute-start(bf16[64,1024]{1,0:T(8,128)(2,1)S(1)} %get-tuple-element.36), channel_id=1, source_target_pairs={{0,128},{1,129},{2,130},{3,131},{4,132},{5,133},{6,134},{7,135},{8... | collective-permute-start | bytes 393224 | tf_op jit(solution)/shard_map/ppermute | solution.py:40
  12.7 1.2 collective-permute-start.3
  13.8 3.5 %collective-permute-done.1.a_ref = bf16[64,1024]{1,0:T(8,128)(2,1)S(1)} collective-permute-done((bf16[64,1024]{1,0:T(8,128)(2,1)S(1)}, bf16[64,1024]{1,0:T(8,128)(2,1)S(1)}, u32[]{:S(2)}, u32[]{:S(2)}) %collective-permute-start.1) | collective-permute-done | bytes 131104 | tf_op jit(solution)/shard_map/ppermute | solution.py:40
  17.3 1.4 %collective-permute-done.2.b_ref = bf16[64,1024]{1,0:T(8,128)(2,1)S(1)} collective-permute-done((bf16[64,1024]{1,0:T(8,128)(2,1)S(1)}, bf16[64,1024]{1,0:T(8,128)(2,1)S(1)}, u32[]{:S(2)}, u32[]{:S(2)}) %collective-permute-start.2) | collective-permute-done | bytes 131104 | tf_op jit(solution)/shard_map/ppermute | solution.py:40
  19.8 3.5 %collective-permute-start.6 = (bf16[64,1024]{1,0:T(8,128)(2,1)S(1)}, bf16[64,1024]{1,0:T(8,128)(2,1)S(1)}, u32[]{:S(2)}, u32[]{:S(2)}) collective-permute-start(bf16[64,1024]{1,0:T(8,128)(2,1)S(1)} %shard_map.88.a_ref.summed_ref.refs_0_.sum_ref), channel_id=1, source_target_pairs={{0,192},{1,193},{2,194},{3,195},{4,196},{5,197},{6,198},{7,199},{8... | collective-permute-start | bytes 393224 | tf_op jit(solution)/shard_map/ppermute | solution.py:40
  24.0 4.6 %collective-permute-done.6.d_ref.refs_3_ = bf16[64,1024]{1,0:T(8,128)(2,1)S(1)} collective-permute-done((bf16[64,1024]{1,0:T(8,128)(2,1)S(1)}, bf16[64,1024]{1,0:T(8,128)(2,1)S(1)}, u32[]{:S(2)}, u32[]{:S(2)}) %collective-permute-start.6) | collective-permute-done | bytes 131104 | tf_op jit(solution)/shard_map/ppermute | solution.py:40
  29.1 3.3 %collective-permute-done.4.b_ref.refs_1_ = bf16[64,1024]{1,0:T(8,128)(2,1)S(1)} collective-permute-done((bf16[64,1024]{1,0:T(8,128)(2,1)S(1)}, bf16[64,1024]{1,0:T(8,128)(2,1)S(1)}, u32[]{:S(2)}, u32[]{:S(2)}) %collective-permute-start.4) | collective-permute-done | bytes 131104 | tf_op jit(solution)/shard_map/ppermute | solution.py:40
  33.3 1.5 %collective-permute-done.7.refs_4_ = bf16[4,64,1024]{2,1,0:T(8,128)(2,1)S(1)} collective-permute-done((bf16[4,64,1024]{2,1,0:T(8,128)(2,1)S(1)}, bf16[4,64,1024]{2,1,0:T(8,128)(2,1)S(1)}, u32[]{:S(2)}, u32[]{:S(2)}) %collective-permute-start.7) | collective-permute-done | bytes 524320 | tf_op jit(solution)/shard_map/ppermute | solution.py:40
  34.9 3.1 %shard_map.91 = (bf16[4,64,1024]{2,1,0:T(8,128)(2,1)S(1)}, f32[4,64,1024]{2,1,0:T(8,128)S(1)}) custom-call(s32[8]{0:T(128)S(1)} %bitcast.19, bf16[8,96,1024]{2,1,0:T(8,128)(2,1)S(1)} %bitcast.16, bf16[8,96,1024]{2,1,0:T(8,128)(2,1)S(1)} %bitcast.14, bf16[64,1024]{1,0:T(8,128)(2,1)S(1)} %shard_map.88.a_ref.summed_ref.refs_0_.sum_ref, ...), custom_call_target="tpu_custom_call" | custom-call | tf_op jit(solution)/shard_map/pallas_call | solution.py:74
  38.6 1.8 %collective-permute-start.14 = (bf16[2,128,1024]{2,1,0:T(8,128)(2,1)S(1)}, bf16[2,128,1024]{2,1,0:T(8,128)(2,1)S(1)}, u32[]{:S(2)}, u32[]{:S(2)}) collective-permute-start(bf16[2,128,1024]{2,1,0:T(8,128)(2,1)S(1)} %get-tuple-element.47), channel_id=1, source_target_pairs={{0,128},{1,129},{2,130},{3,131},{4,132},{5,133},{6,134},{7,135},{8... | collective-permute-start | bytes 1572872 | tf_op jit(solution)/shard_map/ppermute | solution.py:40
  42.2 1.9 %collective-permute-start.10 = (bf16[64,1024]{1,0:T(8,128)(2,1)S(1)}, bf16[64,1024]{1,0:T(8,128)(2,1)S(1)}, u32[]{:S(2)}, u32[]{:S(2)}) collective-permute-start(bf16[64,1024]{1,0:T(8,128)(2,1)S(1)} %get-tuple-element.42), channel_id=1, source_target_pairs={{0,128},{1,129},{2,130},{3,131},{4,132},{5,133},{6,134},{7,135},{8... | collective-permute-start | bytes 393224 | tf_op jit(solution)/shard_map/ppermute | solution.py:40
  44.1 19.9 %collective-permute-done.13.refs_2_ = bf16[2,128,1024]{2,1,0:T(8,128)(2,1)S(1)} collective-permute-done((bf16[2,128,1024]{2,1,0:T(8,128)(2,1)S(1)}, bf16[2,128,1024]{2,1,0:T(8,128)(2,1)S(1)}, u32[]{:S(2)}, u32[]{:S(2)}) %collective-permute-start.13) | collective-permute-done | bytes 524320 | tf_op jit(solution)/shard_map/ppermute | solution.py:40
  64.1 6.1 %shard_map.90.inverse_ref = f32[64,64]{1,0:T(8,128)S(1)} custom-call(bf16[64,1024]{1,0:T(8,128)(2,1)S(1)} %shard_map.88.a_ref.summed_ref.refs_0_.sum_ref), custom_call_target="tpu_custom_call" | custom-call | tf_op jit(solution)/shard_map/pallas_call | solution.py:74
  70.4 5.6 %shard_map.95 = (bf16[64,1024]{1,0:T(8,128)(2,1)S(1)}, bf16[2,128,640]{2,1,0:T(8,128)(2,1)S(1)}, bf16[2,128,640]{2,1,0:T(8,128)(2,1)S(1)}, bf16[2,128,640]{2,1,0:T(8,128)(2,1)S(1)}, bf16[2,128,640]{2,1,0:T(8,128)(2,1)S(1)}) custom-call(bf16[64,1024]{1,0:T(8,128)(2,1)S(1)} %shard_map.88.a_ref.summed_ref.refs_0_.sum_ref, f32[64,64]{1,0:T(8,128)S(1)} %shard_map.90.inverse_ref, ...), custom_call_target="tpu_custom_call" | custom-call | tf_op jit(solution)/shard_map/pallas_call | solution.py:74
  76.0 2.7 %collective-permute-start.20 = (bf16[2,128,640]{2,1,0:T(8,128)(2,1)S(1)}, bf16[2,128,640]{2,1,0:T(8,128)(2,1)S(1)}, u32[]{:S(2)}, u32[]{:S(2)}) collective-permute-start(bf16[2,128,640]{2,1,0:T(8,128)(2,1)S(1)} %get-tuple-element.50), channel_id=1, source_target_pairs={{0,1},{1,2},{2,3},{3,0},{4,5},{5,6},{6,7},{7,4},{8,9},{9,10},{10,1... | collective-permute-start | bytes 983048 | tf_op jit(solution)/shard_map/ppermute | solution.py:40
  78.7 4.6 %collective-permute-start.21 = (bf16[2,128,640]{2,1,0:T(8,128)(2,1)S(1)}, bf16[2,128,640]{2,1,0:T(8,128)(2,1)S(1)}, u32[]{:S(2)}, u32[]{:S(2)}) collective-permute-start(bf16[2,128,640]{2,1,0:T(8,128)(2,1)S(1)} %get-tuple-element.51), channel_id=1, source_target_pairs={{0,65},{1,66},{2,67},{3,64},{4,69},{5,70},{6,71},{7,68},{8,73},{9,... | collective-permute-start | bytes 983048 | tf_op jit(solution)/shard_map/ppermute | solution.py:40
  83.3 1.9 %collective-permute-start.22 = (bf16[2,128,640]{2,1,0:T(8,128)(2,1)S(1)}, bf16[2,128,640]{2,1,0:T(8,128)(2,1)S(1)}, u32[]{:S(2)}, u32[]{:S(2)}) collective-permute-start(bf16[2,128,640]{2,1,0:T(8,128)(2,1)S(1)} %get-tuple-element.52), channel_id=1, source_target_pairs={{0,129},{1,130},{2,131},{3,128},{4,133},{5,134},{6,135},{7,132},{8... | collective-permute-start | bytes 983048 | tf_op jit(solution)/shard_map/ppermute | solution.py:40
  85.2 3.5 %collective-permute-start.23 = (bf16[2,128,640]{2,1,0:T(8,128)(2,1)S(1)}, bf16[2,128,640]{2,1,0:T(8,128)(2,1)S(1)}, u32[]{:S(2)}, u32[]{:S(2)}) collective-permute-start(bf16[2,128,640]{2,1,0:T(8,128)(2,1)S(1)} %get-tuple-element.53), channel_id=1, source_target_pairs={{0,193},{1,194},{2,195},{3,192},{4,197},{5,198},{6,199},{7,196},{8... | collective-permute-start | bytes 983048 | tf_op jit(solution)/shard_map/ppermute | solution.py:40
  88.7 3.8 %collective-permute-start.18 = (bf16[64,1024]{1,0:T(8,128)(2,1)S(1)}, bf16[64,1024]{1,0:T(8,128)(2,1)S(1)}, u32[]{:S(2)}, u32[]{:S(2)}) collective-permute-start(bf16[64,1024]{1,0:T(8,128)(2,1)S(1)} %get-tuple-element.49.a_ref.refs_5_), channel_id=1, source_target_pairs={{0,192},{1,193},{2,194},{3,195},{4,196},{5,197},{6,198},{7,199},{8... | collective-permute-start | bytes 393224 | tf_op jit(solution)/shard_map/ppermute | solution.py:40
  92.5 1.2 collective-permute-start.17
  93.7 2.1 %collective-permute-start.16 = (bf16[64,1024]{1,0:T(8,128)(2,1)S(1)}, bf16[64,1024]{1,0:T(8,128)(2,1)S(1)}, u32[]{:S(2)}, u32[]{:S(2)}) collective-permute-start(bf16[64,1024]{1,0:T(8,128)(2,1)S(1)} %get-tuple-element.49.a_ref.refs_5_), channel_id=1, source_target_pairs={{0,64},{1,65},{2,66},{3,67},{4,68},{5,69},{6,70},{7,71},{8,72},{9,... | collective-permute-start | bytes 393224 | tf_op jit(solution)/shard_map/ppermute | solution.py:40
  95.8 1.2 collective-permute-done.22.c_ref
  97.0 4.6 %collective-permute-done.23.d_ref = bf16[2,128,640]{2,1,0:T(8,128)(2,1)S(1)} collective-permute-done((bf16[2,128,640]{2,1,0:T(8,128)(2,1)S(1)}, bf16[2,128,640]{2,1,0:T(8,128)(2,1)S(1)}, u32[]{:S(2)}, u32[]{:S(2)}) %collective-permute-start.23) | collective-permute-done | bytes 327712 | tf_op jit(solution)/shard_map/ppermute | solution.py:40
  102.0 3.2 %collective-permute-start.24 = (bf16[2,128,640]{2,1,0:T(8,128)(2,1)S(1)}, bf16[2,128,640]{2,1,0:T(8,128)(2,1)S(1)}, u32[]{:S(2)}, u32[]{:S(2)}) collective-permute-start(bf16[2,128,640]{2,1,0:T(8,128)(2,1)S(1)} %get-tuple-element.55), channel_id=1, source_target_pairs={{0,32},{1,33},{2,34},{3,35},{4,36},{5,37},{6,38},{7,39},{8,40},{9,... | collective-permute-start | bytes 983048 | tf_op jit(solution)/shard_map/ppermute | solution.py:40
  105.3 1.2 collective-permute-start.19
  106.6 2.1 %collective-permute-start.25 = (bf16[128,640]{1,0:T(8,128)(2,1)S(1)}, bf16[128,640]{1,0:T(8,128)(2,1)S(1)}, u32[]{:S(2)}, u32[]{:S(2)}) collective-permute-start(bf16[128,640]{1,0:T(8,128)(2,1)S(1)} %get-tuple-element.57), channel_id=1, source_target_pairs={{0,4},{1,5},{2,6},{3,7},{4,8},{5,9},{6,10},{7,11},{8,12},{9,13},{1... | collective-permute-start | bytes 491528 | tf_op jit(solution)/shard_map/ppermute | solution.py:40
  108.7 8.2 %collective-permute-done.25.onward_ref = bf16[128,640]{1,0:T(8,128)(2,1)S(1)} collective-permute-done((bf16[128,640]{1,0:T(8,128)(2,1)S(1)}, bf16[128,640]{1,0:T(8,128)(2,1)S(1)}, u32[]{:S(2)}, u32[]{:S(2)}) %collective-permute-start.25) | collective-permute-done | bytes 163872 | tf_op jit(solution)/shard_map/ppermute | solution.py:40
  117.6 3.0 %collective-permute-start.27 = (bf16[128,128]{1,0:T(8,128)(2,1)S(1)}, bf16[128,128]{1,0:T(8,128)(2,1)S(1)}, u32[]{:S(2)}, u32[]{:S(2)}) collective-permute-start(bf16[128,128]{1,0:T(8,128)(2,1)S(1)} %get-tuple-element.60), channel_id=1, source_target_pairs={{0,192},{1,193},{2,194},{3,195},{4,196},{5,197},{6,198},{7,199},{8... | collective-permute-start | bytes 98312 | tf_op jit(solution)/shard_map/ppermute | solution.py:40
  120.8 4.0 %shard_map.97 = bf16[8,128,1024]{2,1,0:T(8,128)(2,1)} custom-call(bf16[8,128,1024]{2,1,0:T(8,128)(2,1)S(1)} %bitcast.12, bf16[1024,1024]{1,0:T(8,128)(2,1)S(1)} %bitcast.10, bf16[64,1024]{1,0:T(8,128)(2,1)S(1)} %shard_map.88.a_ref.summed_ref.refs_0_.sum_ref, bf16[64,1024]{1,0:T(8,128)(2,1)S(1)} %collective-permute-done.4.b_ref.refs_1_, ...), custom_call_target="tpu_custom_call" | custom-call | tf_op jit(solution)/shard_map/pallas_call | solution.py:74
  (54 shorter events, 9.4 us)
Async XLA Ops:
  5.7 4.8 %collective-permute-start = (bf16[4,64,1024]{2,1,0:T(8,128)(2,1)S(1)}, bf16[4,64,1024]{2,1,0:T(8,128)(2,1)S(1)}, u32[]{:S(2)}, u32[]{:S(2)}) collective-permute-start(bf16[4,64,1024]{2,1,0:T(8,128)(2,1)S(1)} %get-tuple-element.33), channel_id=1, source_target_pairs={{0,32},{1,33},{2,34},{3,35},{4,36},{5,37},{6,38},{7,39},{8,40},{9,... | collective-permute-start | bytes 1572872 | tf_op jit(solution)/shard_map/ppermute | solution.py:40
  9.1 25.7 %copy-start.2 = (bf16[1,8,1,96,1024]{4,3,2,1,0:T(8,128)(2,1)S(1)}, bf16[1,8,1,96,1024]{4,3,2,1,0:T(8,128)(2,1)}, u32[]{:S(2)}) copy-start(bf16[1,8,1,96,1024]{4,3,2,1,0:T(8,128)(2,1)} %param.11) | copy-start | bytes 4718596
  9.1 25.7 %copy-start.3 = (bf16[1,8,1,96,1024]{4,3,2,1,0:T(8,128)(2,1)S(1)}, bf16[1,8,1,96,1024]{4,3,2,1,0:T(8,128)(2,1)}, u32[]{:S(2)}) copy-start(bf16[1,8,1,96,1024]{4,3,2,1,0:T(8,128)(2,1)} %param.10) | copy-start | bytes 4718596
  9.2 29.3 %collective-permute-start.12 = (bf16[4,128,1024]{2,1,0:T(8,128)(2,1)S(1)}, bf16[4,128,1024]{2,1,0:T(8,128)(2,1)S(1)}, u32[]{:S(2)}, u32[]{:S(2)}) collective-permute-start(bf16[4,128,1024]{2,1,0:T(8,128)(2,1)S(1)} %get-tuple-element.45), channel_id=1, source_target_pairs={{0,32},{1,33},{2,34},{3,35},{4,36},{5,37},{6,38},{7,39},{8,40},{9,... | collective-permute-start | bytes 3145736 | tf_op jit(solution)/shard_map/ppermute | solution.py:40
  10.6 6.7 %collective-permute-start.1 = (bf16[64,1024]{1,0:T(8,128)(2,1)S(1)}, bf16[64,1024]{1,0:T(8,128)(2,1)S(1)}, u32[]{:S(2)}, u32[]{:S(2)}) collective-permute-start(bf16[64,1024]{1,0:T(8,128)(2,1)S(1)} %get-tuple-element.35), channel_id=1, source_target_pairs={{0,64},{1,65},{2,66},{3,67},{4,68},{5,69},{6,70},{7,71},{8,72},{9,... | collective-permute-start | bytes 393224 | tf_op jit(solution)/shard_map/ppermute | solution.py:40
  10.7 8.0 %collective-permute-start.2 = (bf16[64,1024]{1,0:T(8,128)(2,1)S(1)}, bf16[64,1024]{1,0:T(8,128)(2,1)S(1)}, u32[]{:S(2)}, u32[]{:S(2)}) collective-permute-start(bf16[64,1024]{1,0:T(8,128)(2,1)S(1)} %get-tuple-element.36), channel_id=1, source_target_pairs={{0,128},{1,129},{2,130},{3,131},{4,132},{5,133},{6,134},{7,135},{8... | collective-permute-start | bytes 393224 | tf_op jit(solution)/shard_map/ppermute | solution.py:40
  12.7 7.1 %collective-permute-start.3 = (bf16[64,1024]{1,0:T(8,128)(2,1)S(1)}, bf16[64,1024]{1,0:T(8,128)(2,1)S(1)}, u32[]{:S(2)}, u32[]{:S(2)}) collective-permute-start(bf16[64,1024]{1,0:T(8,128)(2,1)S(1)} %get-tuple-element.37), channel_id=1, source_target_pairs={{0,192},{1,193},{2,194},{3,195},{4,196},{5,197},{6,198},{7,199},{8... | collective-permute-start | bytes 393224 | tf_op jit(solution)/shard_map/ppermute | solution.py:40
  19.8 8.8 %collective-permute-start.6 = (bf16[64,1024]{1,0:T(8,128)(2,1)S(1)}, bf16[64,1024]{1,0:T(8,128)(2,1)S(1)}, u32[]{:S(2)}, u32[]{:S(2)}) collective-permute-start(bf16[64,1024]{1,0:T(8,128)(2,1)S(1)} %shard_map.88.a_ref.summed_ref.refs_0_.sum_ref), channel_id=1, source_target_pairs={{0,192},{1,193},{2,194},{3,195},{4,196},{5,197},{6,198},{7,199},{8... | collective-permute-start | bytes 393224 | tf_op jit(solution)/shard_map/ppermute | solution.py:40
  23.3 5.9 %collective-permute-start.5 = (bf16[64,1024]{1,0:T(8,128)(2,1)S(1)}, bf16[64,1024]{1,0:T(8,128)(2,1)S(1)}, u32[]{:S(2)}, u32[]{:S(2)}) collective-permute-start(bf16[64,1024]{1,0:T(8,128)(2,1)S(1)} %shard_map.88.a_ref.summed_ref.refs_0_.sum_ref), channel_id=1, source_target_pairs={{0,128},{1,129},{2,130},{3,131},{4,132},{5,133},{6,134},{7,135},{8... | collective-permute-start | bytes 393224 | tf_op jit(solution)/shard_map/ppermute | solution.py:40
  23.3 9.1 %collective-permute-start.4 = (bf16[64,1024]{1,0:T(8,128)(2,1)S(1)}, bf16[64,1024]{1,0:T(8,128)(2,1)S(1)}, u32[]{:S(2)}, u32[]{:S(2)}) collective-permute-start(bf16[64,1024]{1,0:T(8,128)(2,1)S(1)} %shard_map.88.a_ref.summed_ref.refs_0_.sum_ref), channel_id=1, source_target_pairs={{0,64},{1,65},{2,66},{3,67},{4,68},{5,69},{6,70},{7,71},{8,72},{9,... | collective-permute-start | bytes 393224 | tf_op jit(solution)/shard_map/ppermute | solution.py:40
  32.5 2.4 %collective-permute-start.7 = (bf16[4,64,1024]{2,1,0:T(8,128)(2,1)S(1)}, bf16[4,64,1024]{2,1,0:T(8,128)(2,1)S(1)}, u32[]{:S(2)}, u32[]{:S(2)}) collective-permute-start(bf16[4,64,1024]{2,1,0:T(8,128)(2,1)S(1)} %shard_map.89), channel_id=1, source_target_pairs={{0,32},{1,33},{2,34},{3,35},{4,36},{5,37},{6,38},{7,39},{8,40},{9,... | collective-permute-start | bytes 1572872 | tf_op jit(solution)/shard_map/ppermute | solution.py:40
  38.0 32.5 %copy-start = (bf16[1,1024,1024]{2,1,0:T(8,128)(2,1)S(1)}, bf16[1,1024,1024]{2,1,0:T(8,128)(2,1)}, u32[]{:S(2)}) copy-start(bf16[1,1024,1024]{2,1,0:T(8,128)(2,1)} %param.9) | copy-start | bytes 6291460
  38.0 3.3 %collective-permute-start.8 = (bf16[4,64,1024]{2,1,0:T(8,128)(2,1)S(1)}, bf16[4,64,1024]{2,1,0:T(8,128)(2,1)S(1)}, u32[]{:S(2)}, u32[]{:S(2)}) collective-permute-start(bf16[4,64,1024]{2,1,0:T(8,128)(2,1)S(1)} %get-tuple-element.39), channel_id=1, source_target_pairs={{0,32},{1,33},{2,34},{3,35},{4,36},{5,37},{6,38},{7,39},{8,40},{9,... | collective-permute-start | bytes 1572872 | tf_op jit(solution)/shard_map/ppermute | solution.py:40
  38.5 25.5 %collective-permute-start.13 = (bf16[2,128,1024]{2,1,0:T(8,128)(2,1)S(1)}, bf16[2,128,1024]{2,1,0:T(8,128)(2,1)S(1)}, u32[]{:S(2)}, u32[]{:S(2)}) collective-permute-start(bf16[2,128,1024]{2,1,0:T(8,128)(2,1)S(1)} %get-tuple-element.46), channel_id=1, source_target_pairs={{0,64},{1,65},{2,66},{3,67},{4,68},{5,69},{6,70},{7,71},{8,72},{9,... | collective-permute-start | bytes 1572872 | tf_op jit(solution)/shard_map/ppermute | solution.py:40
  38.6 31.5 %collective-permute-start.14 = (bf16[2,128,1024]{2,1,0:T(8,128)(2,1)S(1)}, bf16[2,128,1024]{2,1,0:T(8,128)(2,1)S(1)}, u32[]{:S(2)}, u32[]{:S(2)}) collective-permute-start(bf16[2,128,1024]{2,1,0:T(8,128)(2,1)S(1)} %get-tuple-element.47), channel_id=1, source_target_pairs={{0,128},{1,129},{2,130},{3,131},{4,132},{5,133},{6,134},{7,135},{8... | collective-permute-start | bytes 1572872 | tf_op jit(solution)/shard_map/ppermute | solution.py:40
  40.4 29.7 %collective-permute-start.15 = (bf16[2,128,1024]{2,1,0:T(8,128)(2,1)S(1)}, bf16[2,128,1024]{2,1,0:T(8,128)(2,1)S(1)}, u32[]{:S(2)}, u32[]{:S(2)}) collective-permute-start(bf16[2,128,1024]{2,1,0:T(8,128)(2,1)S(1)} %get-tuple-element.48), channel_id=1, source_target_pairs={{0,192},{1,193},{2,194},{3,195},{4,196},{5,197},{6,198},{7,199},{8... | collective-permute-start | bytes 1572872 | tf_op jit(solution)/shard_map/ppermute | solution.py:40
  41.4 28.8 %collective-permute-start.9 = (bf16[64,1024]{1,0:T(8,128)(2,1)S(1)}, bf16[64,1024]{1,0:T(8,128)(2,1)S(1)}, u32[]{:S(2)}, u32[]{:S(2)}) collective-permute-start(bf16[64,1024]{1,0:T(8,128)(2,1)S(1)} %get-tuple-element.41), channel_id=1, source_target_pairs={{0,64},{1,65},{2,66},{3,67},{4,68},{5,69},{6,70},{7,71},{8,72},{9,... | collective-permute-start | bytes 393224 | tf_op jit(solution)/shard_map/ppermute | solution.py:40
  42.2 27.9 %collective-permute-start.10 = (bf16[64,1024]{1,0:T(8,128)(2,1)S(1)}, bf16[64,1024]{1,0:T(8,128)(2,1)S(1)}, u32[]{:S(2)}, u32[]{:S(2)}) collective-permute-start(bf16[64,1024]{1,0:T(8,128)(2,1)S(1)} %get-tuple-element.42), channel_id=1, source_target_pairs={{0,128},{1,129},{2,130},{3,131},{4,132},{5,133},{6,134},{7,135},{8... | collective-permute-start | bytes 393224 | tf_op jit(solution)/shard_map/ppermute | solution.py:40
  64.1 6.4 %collective-permute-start.11 = (bf16[64,1024]{1,0:T(8,128)(2,1)S(1)}, bf16[64,1024]{1,0:T(8,128)(2,1)S(1)}, u32[]{:S(2)}, u32[]{:S(2)}) collective-permute-start(bf16[64,1024]{1,0:T(8,128)(2,1)S(1)} %get-tuple-element.43), channel_id=1, source_target_pairs={{0,192},{1,193},{2,194},{3,195},{4,196},{5,197},{6,198},{7,199},{8... | collective-permute-start | bytes 393224 | tf_op jit(solution)/shard_map/ppermute | solution.py:40
  76.0 16.5 %collective-permute-start.20 = (bf16[2,128,640]{2,1,0:T(8,128)(2,1)S(1)}, bf16[2,128,640]{2,1,0:T(8,128)(2,1)S(1)}, u32[]{:S(2)}, u32[]{:S(2)}) collective-permute-start(bf16[2,128,640]{2,1,0:T(8,128)(2,1)S(1)} %get-tuple-element.50), channel_id=1, source_target_pairs={{0,1},{1,2},{2,3},{3,0},{4,5},{5,6},{6,7},{7,4},{8,9},{9,10},{10,1... | collective-permute-start | bytes 983048 | tf_op jit(solution)/shard_map/ppermute | solution.py:40
  78.7 15.0 %collective-permute-start.21 = (bf16[2,128,640]{2,1,0:T(8,128)(2,1)S(1)}, bf16[2,128,640]{2,1,0:T(8,128)(2,1)S(1)}, u32[]{:S(2)}, u32[]{:S(2)}) collective-permute-start(bf16[2,128,640]{2,1,0:T(8,128)(2,1)S(1)} %get-tuple-element.51), channel_id=1, source_target_pairs={{0,65},{1,66},{2,67},{3,64},{4,69},{5,70},{6,71},{7,68},{8,73},{9,... | collective-permute-start | bytes 983048 | tf_op jit(solution)/shard_map/ppermute | solution.py:40
  83.3 13.7 %collective-permute-start.22 = (bf16[2,128,640]{2,1,0:T(8,128)(2,1)S(1)}, bf16[2,128,640]{2,1,0:T(8,128)(2,1)S(1)}, u32[]{:S(2)}, u32[]{:S(2)}) collective-permute-start(bf16[2,128,640]{2,1,0:T(8,128)(2,1)S(1)} %get-tuple-element.52), channel_id=1, source_target_pairs={{0,129},{1,130},{2,131},{3,128},{4,133},{5,134},{6,135},{7,132},{8... | collective-permute-start | bytes 983048 | tf_op jit(solution)/shard_map/ppermute | solution.py:40
  85.2 16.3 %collective-permute-start.23 = (bf16[2,128,640]{2,1,0:T(8,128)(2,1)S(1)}, bf16[2,128,640]{2,1,0:T(8,128)(2,1)S(1)}, u32[]{:S(2)}, u32[]{:S(2)}) collective-permute-start(bf16[2,128,640]{2,1,0:T(8,128)(2,1)S(1)} %get-tuple-element.53), channel_id=1, source_target_pairs={{0,193},{1,194},{2,195},{3,192},{4,197},{5,198},{6,199},{7,196},{8... | collective-permute-start | bytes 983048 | tf_op jit(solution)/shard_map/ppermute | solution.py:40
  88.7 16.6 %collective-permute-start.18 = (bf16[64,1024]{1,0:T(8,128)(2,1)S(1)}, bf16[64,1024]{1,0:T(8,128)(2,1)S(1)}, u32[]{:S(2)}, u32[]{:S(2)}) collective-permute-start(bf16[64,1024]{1,0:T(8,128)(2,1)S(1)} %get-tuple-element.49.a_ref.refs_5_), channel_id=1, source_target_pairs={{0,192},{1,193},{2,194},{3,195},{4,196},{5,197},{6,198},{7,199},{8... | collective-permute-start | bytes 393224 | tf_op jit(solution)/shard_map/ppermute | solution.py:40
  92.5 12.8 %collective-permute-start.17 = (bf16[64,1024]{1,0:T(8,128)(2,1)S(1)}, bf16[64,1024]{1,0:T(8,128)(2,1)S(1)}, u32[]{:S(2)}, u32[]{:S(2)}) collective-permute-start(bf16[64,1024]{1,0:T(8,128)(2,1)S(1)} %get-tuple-element.49.a_ref.refs_5_), channel_id=1, source_target_pairs={{0,128},{1,129},{2,130},{3,131},{4,132},{5,133},{6,134},{7,135},{8... | collective-permute-start | bytes 393224 | tf_op jit(solution)/shard_map/ppermute | solution.py:40
  93.7 11.6 %collective-permute-start.16 = (bf16[64,1024]{1,0:T(8,128)(2,1)S(1)}, bf16[64,1024]{1,0:T(8,128)(2,1)S(1)}, u32[]{:S(2)}, u32[]{:S(2)}) collective-permute-start(bf16[64,1024]{1,0:T(8,128)(2,1)S(1)} %get-tuple-element.49.a_ref.refs_5_), channel_id=1, source_target_pairs={{0,64},{1,65},{2,66},{3,67},{4,68},{5,69},{6,70},{7,71},{8,72},{9,... | collective-permute-start | bytes 393224 | tf_op jit(solution)/shard_map/ppermute | solution.py:40
  102.0 4.5 %collective-permute-start.24 = (bf16[2,128,640]{2,1,0:T(8,128)(2,1)S(1)}, bf16[2,128,640]{2,1,0:T(8,128)(2,1)S(1)}, u32[]{:S(2)}, u32[]{:S(2)}) collective-permute-start(bf16[2,128,640]{2,1,0:T(8,128)(2,1)S(1)} %get-tuple-element.55), channel_id=1, source_target_pairs={{0,32},{1,33},{2,34},{3,35},{4,36},{5,37},{6,38},{7,39},{8,40},{9,... | collective-permute-start | bytes 983048 | tf_op jit(solution)/shard_map/ppermute | solution.py:40
  105.3 15.4 %collective-permute-start.19 = (bf16[4,64,1024]{2,1,0:T(8,128)(2,1)S(1)}, bf16[4,64,1024]{2,1,0:T(8,128)(2,1)S(1)}, u32[]{:S(2)}, u32[]{:S(2)}) collective-permute-start(bf16[4,64,1024]{2,1,0:T(8,128)(2,1)S(1)} %shard_map.96), channel_id=1, source_target_pairs={{0,32},{1,33},{2,34},{3,35},{4,36},{5,37},{6,38},{7,39},{8,40},{9,... | collective-permute-start | bytes 1572872 | tf_op jit(solution)/shard_map/ppermute | solution.py:40
  106.6 10.3 %collective-permute-start.25 = (bf16[128,640]{1,0:T(8,128)(2,1)S(1)}, bf16[128,640]{1,0:T(8,128)(2,1)S(1)}, u32[]{:S(2)}, u32[]{:S(2)}) collective-permute-start(bf16[128,640]{1,0:T(8,128)(2,1)S(1)} %get-tuple-element.57), channel_id=1, source_target_pairs={{0,4},{1,5},{2,6},{3,7},{4,8},{5,9},{6,10},{7,11},{8,12},{9,13},{1... | collective-permute-start | bytes 491528 | tf_op jit(solution)/shard_map/ppermute | solution.py:40
  117.0 7.8 %collective-permute-start.26 = (bf16[128,128]{1,0:T(8,128)(2,1)S(1)}, bf16[128,128]{1,0:T(8,128)(2,1)S(1)}, u32[]{:S(2)}, u32[]{:S(2)}) collective-permute-start(bf16[128,128]{1,0:T(8,128)(2,1)S(1)} %get-tuple-element.59), channel_id=1, source_target_pairs={{0,224},{1,225},{2,226},{3,227},{4,228},{5,229},{6,230},{7,231},{8... | collective-permute-start | bytes 98312 | tf_op jit(solution)/shard_map/ppermute | solution.py:40
  117.6 7.2 %collective-permute-start.27 = (bf16[128,128]{1,0:T(8,128)(2,1)S(1)}, bf16[128,128]{1,0:T(8,128)(2,1)S(1)}, u32[]{:S(2)}, u32[]{:S(2)}) collective-permute-start(bf16[128,128]{1,0:T(8,128)(2,1)S(1)} %get-tuple-element.60), channel_id=1, source_target_pairs={{0,192},{1,193},{2,194},{3,195},{4,196},{5,197},{6,198},{7,199},{8... | collective-permute-start | bytes 98312 | tf_op jit(solution)/shard_map/ppermute | solution.py:40
  120.6 4.8 %collective-permute-start.28 = (bf16[128,128]{1,0:T(8,128)(2,1)S(1)}, bf16[128,128]{1,0:T(8,128)(2,1)S(1)}, u32[]{:S(2)}, u32[]{:S(2)}) collective-permute-start(bf16[128,128]{1,0:T(8,128)(2,1)S(1)} %get-tuple-element.61), channel_id=1, source_target_pairs={{0,160},{1,161},{2,162},{3,163},{4,164},{5,165},{6,166},{7,167},{8... | collective-permute-start | bytes 98312 | tf_op jit(solution)/shard_map/ppermute | solution.py:40
  (3 other events, 38.9 us)
